TPU v7x, 512 devices: a whole 4x4x16 slice. The times are simulated.
512 devices in a mesh: gx: 32 (over z, core), gy: 16 (over y, x).
Axes of the slice: x: 4, y: 4, z: 16, core: 2. Of those that a mesh axis runs over, the one named last changes fastest.
Arguments:
- patches: bfloat16 [512, 6144], P('gy', 'gx'), may hold values from -40 to 40
- ln_gain: float32 [6144], P('gx'), may hold values from 0.5 to 1.5
- weight_in: bfloat16 [6144, 24576], P('gx', 'gy'), may hold values from -0.12757759 to 0.12757759
- weight_out: bfloat16 [24576, 6144], P('gy', 'gx'), may hold values from -0.063788795 to 0.063788795
- upstream: bfloat16 [512, 6144], P('gy', 'gx'), may hold values from -18 to 18
- row_in: float32 [6144], P('gx'), may hold values from 7.68 to 92.16
- col_in: float32 [24576], P('gy'), may hold values from 7.68 to 92.16
- row_out: float32 [24576], P('gy'), may hold values from 7.68 to 92.16
- col_out: float32 [6144], P('gx'), may hold values from 7.68 to 92.16
Outputs:
- output: bfloat16 [512, 6144], P('gy', 'gx')
- input_grad: float32 [512, 6144], P('gy', 'gx')
- update_in: float32 [6144, 24576], P('gx', 'gy')
- update_out: float32 [24576, 6144], P('gy', 'gx')
All inputs are finite; a program needn't handle non-finite values.
Results may differ from a plain program's by a relative error of at most 0.028.
Values may be sent and summed in bfloat16 or wider, within the bound.
A program may use at most 64 MiB of HBM per device.

v0:
```python
import functools

import jax
import jax.numpy as jnp
from jax import lax
from jax.sharding import Mesh
from jax.sharding import PartitionSpec as P

D = 6144
FF = 24576
GX = ("gx_0", "gx_1")
GY = ("gy_0", "gy_1")
GX_GY = ("gx_0", "gx_1", "gy_0", "gy_1")


def sent_to_all(array, axis):
    copies = jnp.broadcast_to(array, (lax.axis_size(axis), *array.shape))
    return lax.all_to_all(copies, axis, split_axis=0, concat_axis=0, tiled=True)


def of_everyone(array, axis):
    everything = sent_to_all(array, axis)
    return jnp.sum(everything, axis=0)


def together(arrays, axis):
    ends = [0]
    for a in arrays:
        ends.append(ends[-1] + a.size)
    total = of_everyone(jnp.concatenate([a.ravel() for a in arrays]), axis)
    return tuple((total[b:e].reshape(a.shape) for a, b, e in zip(arrays, ends, ends[1:])))


def laid_out(blocks, dim):
    dims = list(blocks.shape[1:])
    dims[dim] *= blocks.shape[0]
    return jnp.moveaxis(blocks, 0, dim).reshape(dims)


def gather_directly(array, axis, dim):
    blocks = sent_to_all(array, axis)
    return laid_out(blocks, dim)


def reduced_to_own(blocks, axes, sequence):
    inside = blocks.shape[1:]
    blocks = blocks.reshape(*(lax.axis_size(a) for a in axes), *inside)
    blocks = jnp.moveaxis(blocks, sequence, range(len(axes))).reshape(-1, *inside)
    for k in sequence:
        blocks = lax.psum_scatter(blocks, axes[k], scatter_dimension=0, tiled=True)
    return blocks[0]


def split_up(array, dim, count):
    before, after = (array.shape[:dim], array.shape[dim + 1 :])
    return jnp.moveaxis(array.reshape(*before, count, -1, *after), dim, 0)


def sum_by_axis(array, axes, sequence, dim):
    count = lax.axis_size(axes)
    return reduced_to_own(split_up(array, dim, count), axes, sequence)


def gather_in_order(array, axes, sequence):
    blocks = array
    for k in sequence:
        blocks = lax.all_gather(blocks, axes[k])
    done = sequence[::-1]
    back = [done.index(k) for k in range(len(axes))]
    blocks = blocks.transpose(*back, *range(len(axes), blocks.ndim))
    return blocks.reshape(-1, *array.shape)


def gather_axes(array, axes, sequence, dim):
    return laid_out(gather_in_order(array, axes, sequence), dim)


def summed_on_arrival(array, axis, dim):
    count = lax.axis_size(axis)
    blocks = lax.all_to_all(split_up(array, dim, count), axis, 0, 0, tiled=True)
    return jnp.sum(blocks.astype(jnp.float32), axis=0)


def over_axes(array, axes):
    return functools.reduce(lax.psum, axes, array)


def contract(left, right, left_dim, right_dim):
    return lax.dot_general(
        left, right, (((left_dim,), (right_dim,)), ((), ())), preferred_element_type=jnp.float32
    )


def rounded_once(values):
    return lax.optimization_barrier(values.astype(jnp.bfloat16)).astype(jnp.float32)


def gelu_parts(summed):
    hidden_pre = rounded_once(summed)
    phi = 0.5 * (1.0 + lax.erf(hidden_pre * 0.7071067811865476))
    slope = phi + hidden_pre * jnp.exp(-0.5 * hidden_pre * hidden_pre) * 0.3989422804014327
    return ((hidden_pre * phi).astype(jnp.bfloat16), slope)


def body(patches, ln_gain, weight_in, weight_out, upstream, row_in, col_in, row_out, col_out):
    x_float = patches.astype(jnp.float32)
    row_sums, row_squares = together(
        (jnp.sum(x_float, axis=1), jnp.sum(x_float * x_float, axis=1)), GX
    )
    row_mean = row_sums / D
    row_var = row_squares / D - row_mean * row_mean
    inv_std = lax.rsqrt(row_var + 1e-06)[:, None]
    unit = (x_float - row_mean[:, None]) * inv_std
    normed = (unit * ln_gain[None, :]).astype(jnp.bfloat16)
    normed_full = gather_directly(normed, GY, 0)
    summed_pre = sum_by_axis(
        jnp.dot(normed_full, weight_in, preferred_element_type=jnp.float32).astype(jnp.bfloat16),
        GX,
        (1, 0),
        0,
    ).astype(jnp.float32)
    hidden, slope = gelu_parts(summed_pre)
    hidden_full = gather_axes(hidden, GX, (0, 1), 0)
    branch = summed_on_arrival(
        jnp.dot(hidden_full, weight_out, preferred_element_type=jnp.float32).astype(jnp.bfloat16),
        GY,
        0,
    )
    output = (x_float + branch).astype(jnp.bfloat16)
    upstream_full = gather_directly(upstream, GY, 0)
    grad_out = contract(hidden_full, upstream_full, 0, 0)
    hidden_grad = rounded_once(
        summed_on_arrival(contract(upstream_full, weight_out, 1, 1).astype(jnp.bfloat16), GX, 0)
    )
    act_grad = (hidden_grad * slope).astype(jnp.bfloat16)
    act_full = gather_axes(act_grad, GX, (0, 1), 0)
    grad_in = contract(normed_full, act_full, 0, 0)
    normed_grad = summed_on_arrival(contract(act_full, weight_in, 1, 1).astype(jnp.bfloat16), GY, 0)
    scaled = normed_grad * ln_gain[None, :]
    first_sum, second_sum = together((jnp.sum(scaled, axis=1), jnp.sum(scaled * unit, axis=1)), GX)
    input_grad = upstream.astype(jnp.float32) + inv_std * (
        scaled - first_sum[:, None] / D - unit * (second_sum[:, None] / D)
    )
    squares_in = grad_in * grad_in + 1e-30
    squares_out = grad_out * grad_out + 1e-30
    row_in_sum, col_out_sum = (
        over_axes(jnp.sum(squares_in, axis=1), GY),
        over_axes(jnp.sum(squares_out, axis=0), GY),
    )
    col_in_sum, row_out_sum = together(
        (jnp.sum(squares_in, axis=0), jnp.sum(squares_out, axis=1)), GX
    )
    row_in_new = 0.9 * row_in + 0.1 * (row_in_sum / FF)
    col_in_new = 0.9 * col_in + 0.1 * (col_in_sum / D)
    row_out_new = 0.9 * row_out + 0.1 * (row_out_sum / D)
    col_out_new = 0.9 * col_out + 0.1 * (col_out_sum / FF)
    total_in, total_out = (
        over_axes(jnp.sum(row_in_new) / lax.axis_size(GY), GX_GY),
        over_axes(jnp.sum(row_out_new) / lax.axis_size(GX), GX_GY),
    )
    mean_in = total_in / D
    mean_out = total_out / FF
    update_in = grad_in / jnp.sqrt(row_in_new[:, None] * col_in_new[None, :] / mean_in)
    update_out = grad_out / jnp.sqrt(row_out_new[:, None] * col_out_new[None, :] / mean_out)
    return (output, input_grad, update_in, update_out)


def solution(mesh):
    split = Mesh(mesh.devices.reshape(16, 2, 4, 4), ("gx_0", "gx_1", "gy_0", "gy_1"))
    placed = (P(GY, GX), P(GX), P(GX, GY), P(GY, GX), P(GY, GX), P(GX), P(GY), P(GY), P(GX))
    return jax.shard_map(
        body,
        mesh=split,
        in_specs=placed,
        out_specs=(P(GY, GX), P(GY, GX), P(GX, GY), P(GY, GX)),
        check_vma=False,
    )
```

profile of v0, /device:TPU:1, one launch (start us, length us, event | category | flops | bytes accessed | tf_op | source)
XLA Modules:
  0.0 401.6 jit_solution(6777684401316600401)
XLA Ops:
  8.2 28.4 %all_to_all.43 = f32[32,1,64]{2,1,0:T(1,128)S(1)} all-to-all(f32[32,1,64]{2,1,0:T(1,128)S(1)} %broadcast_in_dim.10), channel_id=1, replica_groups=mesh['gx_0'=16,'gx_1'=2,'gy_0'=4,'gy_1'=4] {'gx_0','gx_1'}, dimensions={0} | all-to-all | bytes 16384 | tf_op jit(solution)/shard_map/all_to_all | solution.py:18
  38.0 6.8 %all-to-all-start.3 = ((bf16[16,32,192]{2,1,0:T(8,128)(2,1)}), bf16[16,32,192]{2,1,0:T(8,128)(2,1)S(1)}, u32[]{:S(2)}, u32[]{:S(2)}) async-start(bf16[16,32,192]{2,1,0:T(8,128)(2,1)} %broadcast_in_dim.12), calls=%async_computation.5 | async-start | bytes 524288 | tf_op jit(solution)/shard_map/all_to_all | solution.py:18
  45.7 6.7 %all-to-all-done.3 = bf16[16,32,192]{2,1,0:T(8,128)(2,1)S(1)} async-done(((bf16[16,32,192]{2,1,0:T(8,128)(2,1)}), bf16[16,32,192]{2,1,0:T(8,128)(2,1)S(1)}, u32[]{:S(2)}, u32[]{:S(2)}) %all-to-all-start.3) | async-done | bytes 196640 | tf_op jit(solution)/shard_map/all_to_all | solution.py:18
  58.5 5.8 %all-to-all-done.1 = bf16[16,32,192]{2,1,0:T(8,128)(2,1)S(1)} async-done(((bf16[16,32,192]{2,1,0:T(8,128)(2,1)}), bf16[16,32,192]{2,1,0:T(8,128)(2,1)S(1)}, u32[]{:S(2)}, u32[]{:S(2)}) %all-to-all-start.1) | async-done | bytes 196640 | tf_op jit(solution)/shard_map/all_to_all | solution.py:18
  64.2 7.0 %all-to-all-start.4 = ((bf16[32,16,1536]{2,1,0:T(8,128)(2,1)}), bf16[32,16,1536]{2,1,0:T(8,128)(2,1)S(1)}, u32[]{:S(2)}, u32[]{:S(2)}) async-start(bf16[32,16,1536]{2,1,0:T(8,128)(2,1)} %bitcast.34), calls=%async_computation.6 | async-start | bytes 3145728 | tf_op jit(solution)/shard_map/all_to_all | solution.py:80
  73.2 19.3 %reduce-scatter.3.cloned.1.call-done = bf16[16,16,1536]{2,1,0:T(8,128)(2,1)} async-done(((bf16[32,16,1536]{2,1,0:T(8,128)(2,1)}), bf16[16,16,1536]{2,1,0:T(8,128)(2,1)}) %reduce-scatter.3.cloned.1.call-update) | async-done | bytes 786448 | tf_op jit(solution)/shard_map/reduce_scatter | solution.py:50
  92.6 76.9 %reduce-scatter.5.cloned.1.call-done = bf16[1,16,1536]{2,1,0:T(8,128)(2,1)} async-done(((bf16[16,16,1536]{2,1,0:T(8,128)(2,1)}), bf16[1,16,1536]{2,1,0:T(8,128)(2,1)}) %reduce-scatter.5.cloned.1.call-update) | async-done | bytes 49168 | tf_op jit(solution)/shard_map/reduce_scatter | solution.py:50
  170.4 27.9 %all-gather.2 = bf16[256,1536]{1,0:T(8,128)(2,1)} all-gather(bf16[16,1536]{1,0:T(8,128)(2,1)S(1)} %get-tuple-element.26), channel_id=4, replica_groups=mesh['gx_0'=16,'gx_1'=2,'gy_0'=4,'gy_1'=4] {'gx_0'}, dimensions={0}, use_global_device_ids=true | all-gather | bytes 835584 | tf_op jit(solution)/shard_map/all_gather | solution.py:67
  198.4 27.0 %all-gather = bf16[256,1536]{1,0:T(8,128)(2,1)} all-gather(bf16[16,1536]{1,0:T(8,128)(2,1)S(1)} %get-tuple-element.27), channel_id=2, replica_groups=mesh['gx_0'=16,'gx_1'=2,'gy_0'=4,'gy_1'=4] {'gx_0'}, dimensions={0}, use_global_device_ids=true | all-gather | bytes 835584 | tf_op jit(solution)/shard_map/all_gather | solution.py:67
  225.3 5.4 %all-gather.9.cloned.1.call-done = bf16[32,16,1536]{2,1,0:T(8,128)(2,1)} async-done(((bf16[16,16,1536]{2,1,0:T(8,128)(2,1)}), bf16[32,16,1536]{2,1,0:T(8,128)(2,1)}) %all-gather.9.cloned.1.call-update) | async-done | bytes 1572880 | tf_op jit(solution)/shard_map/all_gather | solution.py:67
  233.8 5.6 %all-to-all-start.5 = ((bf16[16,32,192]{2,1,0:T(8,128)(2,1)}), bf16[16,32,192]{2,1,0:T(8,128)(2,1)}, u32[]{:S(2)}, u32[]{:S(2)}) async-start(bf16[16,32,192]{2,1,0:T(8,128)(2,1)} %bitcast.17), calls=%async_computation.7 | async-start | bytes 524288 | tf_op jit(solution)/shard_map/all_to_all | solution.py:80
  241.5 22.6 %all-gather.7.cloned.1.call-done = bf16[32,16,1536]{2,1,0:T(8,128)(2,1)} async-done(((bf16[16,16,1536]{2,1,0:T(8,128)(2,1)}), bf16[32,16,1536]{2,1,0:T(8,128)(2,1)}) %all-gather.7.cloned.1.call-update) | async-done | bytes 1572880 | tf_op jit(solution)/shard_map/all_gather | solution.py:67
  269.7 5.7 %all-to-all-start.2 = ((bf16[16,32,192]{2,1,0:T(8,128)(2,1)}), bf16[16,32,192]{2,1,0:T(8,128)(2,1)S(1)}, u32[]{:S(2)}, u32[]{:S(2)}) async-start(bf16[16,32,192]{2,1,0:T(8,128)(2,1)} %bitcast.49), calls=%async_computation.4 | async-start | bytes 524288 | tf_op jit(solution)/shard_map/all_to_all | solution.py:80
  276.8 6.9 %all-to-all-done.2 = bf16[16,32,192]{2,1,0:T(8,128)(2,1)S(1)} async-done(((bf16[16,32,192]{2,1,0:T(8,128)(2,1)}), bf16[16,32,192]{2,1,0:T(8,128)(2,1)S(1)}, u32[]{:S(2)}, u32[]{:S(2)}) %all-to-all-start.2) | async-done | bytes 196640 | tf_op jit(solution)/shard_map/all_to_all | solution.py:80
  284.3 13.7 %all-to-all-start.6 = ((f32[32,1,64]{2,1,0:T(1,128)}), f32[32,1,64]{2,1,0:T(1,128)S(1)}, u32[]{:S(2)}, u32[]{:S(2)}) async-start(f32[32,1,64]{2,1,0:T(1,128)} %broadcast_in_dim.13), calls=%async_computation.8 | async-start | bytes 32768 | tf_op jit(solution)/shard_map/all_to_all | solution.py:18
  298.0 11.7 %all-to-all-done.6 = f32[32,1,64]{2,1,0:T(1,128)S(1)} async-done(((f32[32,1,64]{2,1,0:T(1,128)}), f32[32,1,64]{2,1,0:T(1,128)S(1)}, u32[]{:S(2)}, u32[]{:S(2)}) %all-to-all-start.6) | async-done | bytes 8224 | tf_op jit(solution)/shard_map/all_to_all | solution.py:18
  310.7 4.4 %all-to-all-start.7 = ((f32[32,1,3072]{2,1,0:T(1,128)}), f32[32,1,3072]{2,1,0:T(1,128)S(1)}, u32[]{:S(2)}, u32[]{:S(2)}) async-start(f32[32,1,3072]{2,1,0:T(1,128)} %broadcast_in_dim.14), calls=%async_computation.9 | async-start | bytes 786432 | tf_op jit(solution)/shard_map/all_to_all | solution.py:18
  315.2 6.9 %psum.84 = f32[192]{0:T(256)S(1)} all-reduce(f32[192]{0:T(256)S(1)} %copy-done.12), channel_id=1, replica_groups=mesh['gx_0'=16,'gx_1'=2,'gy_0'=4,'gy_1'=4] {'gy_0'}, use_global_device_ids=true, to_apply=%region_12.0 | all-reduce | flops 192 | bytes 1536 | tf_op jit(solution)/shard_map/psum | solution.py:85
  322.0 7.2 %psum.85 = f32[192]{0:T(256)S(1)} all-reduce(f32[192]{0:T(256)S(1)} %psum.84), channel_id=1, replica_groups=mesh['gx_0'=16,'gx_1'=2,'gy_0'=4,'gy_1'=4] {'gy_1'}, use_global_device_ids=true, to_apply=%region_13.0 | all-reduce | flops 192 | bytes 1536 | tf_op jit(solution)/shard_map/psum | solution.py:85
  330.6 12.4 %all-to-all-done.7 = f32[32,1,3072]{2,1,0:T(1,128)S(1)} async-done(((f32[32,1,3072]{2,1,0:T(1,128)}), f32[32,1,3072]{2,1,0:T(1,128)S(1)}, u32[]{:S(2)}, u32[]{:S(2)}) %all-to-all-start.7) | async-done | bytes 393248 | tf_op jit(solution)/shard_map/all_to_all | solution.py:18
  345.2 20.7 %all-reduce = (f32[]{:T(128)}, f32[]{:T(128)}) all-reduce(f32[]{:T(128)S(6)} %div.50, f32[]{:T(128)S(6)} %div.55), channel_id=1, replica_groups=mesh['gx_0'=16,'gx_1'=2,'gy_0'=4,'gy_1'=4] {'gx_0'}, use_global_device_ids=true, to_apply=%region_18.0 | all-reduce | flops 2 | bytes 16 | tf_op jit(solution)/shard_map/psum | solution.py:85
  365.9 10.5 %all-reduce.3 = (f32[]{:T(128)}, f32[]{:T(128)}) all-reduce(f32[]{:T(128)} %get-tuple-element.12, f32[]{:T(128)} %get-tuple-element.13), channel_id=1, replica_groups=mesh['gx_0'=16,'gx_1'=2,'gy_0'=4,'gy_1'=4] {'gx_1'}, use_global_device_ids=true, to_apply=%region_19.0 | all-reduce | flops 2 | bytes 16 | tf_op jit(solution)/shard_map/psum | solution.py:85
  376.4 7.2 %all-reduce.2 = (f32[]{:T(128)}, f32[]{:T(128)}, f32[192]{0:T(256)S(1)}) all-reduce(f32[]{:T(128)} %get-tuple-element.20, f32[]{:T(128)} %get-tuple-element.21, f32[192]{0:T(256)S(1)} %get-tuple-element.4), channel_id=1, replica_groups=mesh['gx_0'=16,'gx_1'=2,'gy_0'=4,'gy_1'=4] {'gy_0'}, use_global_device_ids=true, to_apply=%region_20.0 | all-reduce | flops 194 | bytes 1552 | tf_op jit(solution)/shard_map/psum | solution.py:85
  383.6 7.3 %all-reduce.1 = (f32[]{:T(128)}, f32[]{:T(128)}, f32[192]{0:T(256)S(1)}) all-reduce(f32[]{:T(128)} %get-tuple-element.17, f32[]{:T(128)} %get-tuple-element.18, f32[192]{0:T(256)S(1)} %get-tuple-element.19), channel_id=1, replica_groups=mesh['gx_0'=16,'gx_1'=2,'gy_0'=4,'gy_1'=4] {'gy_1'}, use_global_device_ids=true, to_apply=%region_21.0 | all-reduce | flops 194 | bytes 1552 | tf_op jit(solution)/shard_map/psum | solution.py:85
  (78 shorter events, 31.0 us)
Async XLA Ops:
  7.2 64.2 %copy-start = (bf16[192,1536]{1,0:T(8,128)(2,1)S(1)}, bf16[192,1536]{1,0:T(8,128)(2,1)}, u32[]{:S(2)}) copy-start(bf16[192,1536]{1,0:T(8,128)(2,1)} %param.11) | copy-start | bytes 1769476
  7.2 49.5 %copy-start.4 = (bf16[1536,192]{0,1:T(8,128)(2,1)S(1)}, bf16[1536,192]{0,1:T(8,128)(2,1)}, u32[]{:S(2)}) copy-start(bf16[1536,192]{0,1:T(8,128)(2,1)} %param.12) | copy-start | bytes 1769476
  38.0 14.4 %all-to-all-start.3 = ((bf16[16,32,192]{2,1,0:T(8,128)(2,1)}), bf16[16,32,192]{2,1,0:T(8,128)(2,1)S(1)}, u32[]{:S(2)}, u32[]{:S(2)}) async-start(bf16[16,32,192]{2,1,0:T(8,128)(2,1)} %broadcast_in_dim.12), calls=%async_computation.5 | async-start | bytes 524288 | tf_op jit(solution)/shard_map/all_to_all | solution.py:18
  52.4 6.0 %copy-start.3 = (bf16[16,32,192]{2,1,0:T(8,128)(2,1)}, bf16[16,32,192]{2,1,0:T(8,128)(2,1)S(1)}, u32[]{:S(2)}) copy-start(bf16[16,32,192]{2,1,0:T(8,128)(2,1)S(1)} %all-to-all-done.3) | copy-start | bytes 589828
  53.2 11.0 %all-to-all-start.1 = ((bf16[16,32,192]{2,1,0:T(8,128)(2,1)}), bf16[16,32,192]{2,1,0:T(8,128)(2,1)S(1)}, u32[]{:S(2)}, u32[]{:S(2)}) async-start(bf16[16,32,192]{2,1,0:T(8,128)(2,1)} %broadcast_in_dim.11), calls=%async_computation.1 | async-start | bytes 524288 | tf_op jit(solution)/shard_map/all_to_all | solution.py:18
  64.2 7.1 %copy-start.1 = (bf16[16,32,192]{2,1,0:T(8,128)(2,1)}, bf16[16,32,192]{2,1,0:T(8,128)(2,1)S(1)}, u32[]{:S(2)}) copy-start(bf16[16,32,192]{2,1,0:T(8,128)(2,1)S(1)} %all-to-all-done.1) | copy-start | bytes 589828
  64.2 105.3 %all-to-all-start.4 = ((bf16[32,16,1536]{2,1,0:T(8,128)(2,1)}), bf16[32,16,1536]{2,1,0:T(8,128)(2,1)S(1)}, u32[]{:S(2)}, u32[]{:S(2)}) async-start(bf16[32,16,1536]{2,1,0:T(8,128)(2,1)} %bitcast.34), calls=%async_computation.6 | async-start | bytes 3145728 | tf_op jit(solution)/shard_map/all_to_all | solution.py:80
  71.3 21.3 %reduce-scatter.3.cloned.1.call-start = ((), (), s32[]{:S(2)}) async-start(), calls=%async_computation.10 | async-start | bytes 2359296 | tf_op jit(solution)/shard_map/reduce_scatter | solution.py:50
  73.2 96.4 %reduce-scatter.5.cloned.1.call-start = ((), (), s32[]{:S(2)}) async-start(), calls=%async_computation.11 | async-start | bytes 835584 | tf_op jit(solution)/shard_map/reduce_scatter | solution.py:50
  92.6 138.2 %all-gather.9.cloned.1.call-start = ((), (), s32[]{:S(2)}) async-start(), calls=%async_computation.13 | async-start | bytes 2359296 | tf_op jit(solution)/shard_map/all_gather | solution.py:67
  198.3 65.8 %all-gather.7.cloned.1.call-start = ((), (), s32[]{:S(2)}) async-start(), calls=%async_computation.12 | async-start | bytes 2359296 | tf_op jit(solution)/shard_map/all_gather | solution.py:67
  233.8 35.9 %all-to-all-start.5 = ((bf16[16,32,192]{2,1,0:T(8,128)(2,1)}), bf16[16,32,192]{2,1,0:T(8,128)(2,1)}, u32[]{:S(2)}, u32[]{:S(2)}) async-start(bf16[16,32,192]{2,1,0:T(8,128)(2,1)} %bitcast.17), calls=%async_computation.7 | async-start | bytes 524288 | tf_op jit(solution)/shard_map/all_to_all | solution.py:80
  264.1 1.6 copy-start.5
  267.2 9.3 %copy-start.6 = (bf16[32,192]{1,0:T(8,128)(2,1)S(1)}, bf16[32,192]{1,0:T(8,128)(2,1)}, u32[]{:S(2)}) copy-start(bf16[32,192]{1,0:T(8,128)(2,1)} %param.9) | copy-start | bytes 36868
  267.2 9.3 %copy-start.9 = (f32[192]{0:T(256)S(1)}, f32[192]{0:T(256)}, u32[]{:S(2)}) copy-start(f32[192]{0:T(256)} %param.10) | copy-start | bytes 2308
  269.7 45.4 %copy-start.12 = (f32[192]{0:T(256)S(1)}, f32[192]{0:T(256)}, u32[]{:S(2)}) copy-start(f32[192]{0:T(256)} %get-tuple-element.7) | copy-start | bytes 2308
  269.7 59.5 %copy-start.13 = (f32[192]{0:T(256)S(1)}, f32[192]{0:T(256)}, u32[]{:S(2)}) copy-start(f32[192]{0:T(256)} %param.14) | copy-start | bytes 2308
  269.7 14.0 %all-to-all-start.2 = ((bf16[16,32,192]{2,1,0:T(8,128)(2,1)}), bf16[16,32,192]{2,1,0:T(8,128)(2,1)S(1)}, u32[]{:S(2)}, u32[]{:S(2)}) async-start(bf16[16,32,192]{2,1,0:T(8,128)(2,1)} %bitcast.49), calls=%async_computation.4 | async-start | bytes 524288 | tf_op jit(solution)/shard_map/all_to_all | solution.py:80
  275.4 67.8 %copy-start.10 = (f32[1536]{0:T(1024)S(1)}, f32[1536]{0:T(1024)}, u32[]{:S(2)}) copy-start(f32[1536]{0:T(1024)} %param.16) | copy-start | bytes 18436
  275.4 67.8 %copy-start.11 = (f32[1536]{0:T(1024)S(1)}, f32[1536]{0:T(1024)}, u32[]{:S(2)}) copy-start(f32[1536]{0:T(1024)} %param.15) | copy-start | bytes 18436
  275.4 69.1 %copy-start.7 = (bf16[32,192]{1,0:T(8,128)(2,1)S(1)}, bf16[32,192]{1,0:T(8,128)(2,1)}, u32[]{:S(2)}) copy-start(bf16[32,192]{1,0:T(8,128)(2,1)} %param.13) | copy-start | bytes 36868
  276.5 115.8 %copy-start.14 = (f32[192]{0:T(256)S(1)}, f32[192]{0:T(256)}, u32[]{:S(2)}) copy-start(f32[192]{0:T(256)} %param.17) | copy-start | bytes 2308
  284.3 25.4 %all-to-all-start.6 = ((f32[32,1,64]{2,1,0:T(1,128)}), f32[32,1,64]{2,1,0:T(1,128)S(1)}, u32[]{:S(2)}, u32[]{:S(2)}) async-start(f32[32,1,64]{2,1,0:T(1,128)} %broadcast_in_dim.13), calls=%async_computation.8 | async-start | bytes 32768 | tf_op jit(solution)/shard_map/all_to_all | solution.py:18
  310.7 32.3 %all-to-all-start.7 = ((f32[32,1,3072]{2,1,0:T(1,128)}), f32[32,1,3072]{2,1,0:T(1,128)S(1)}, u32[]{:S(2)}, u32[]{:S(2)}) async-start(f32[32,1,3072]{2,1,0:T(1,128)} %broadcast_in_dim.14), calls=%async_computation.9 | async-start | bytes 786432 | tf_op jit(solution)/shard_map/all_to_all | solution.py:18
  (2 other events, 2.3 us)
Sparse Core Ops, SparseCore 0:
  74.9 17.6 reduce-scatter.2
  95.4 74.1 reduce-scatter.4
  198.4 32.3 all-gather.8
  232.7 31.3 all-gather.6
where the time goes:
time: 406 us; the launch traced here: 402 us
  waiting for transfers between devices  168 us (41%)
  blocking collectives  143 us (35%)
  starting transfers between devices  46.8 us (12%)
  between operations  16.7 us (4%)
  local copies, waits for them, and re-layouts  10.7 us (3%)
  matrix products  8.26 us (2%)
  other arithmetic  8.25 us (2%)
    reduce_scatter x2, waiting for transfers between devices, reduced_to_own(): blocks = lax.psum_scatter(blocks, axes[k], scatter_dimension=0, tiled=True)  96.3 us
    psum x6, blocking collectives, over_axes(): return functools.reduce(lax.psum, axes, array)  59.7 us
    all_gather x2, blocking collectives, gather_in_order(): blocks = lax.all_gather(blocks, axes[k])  54.8 us
    all_to_all x4, waiting for transfers between devices, sent_to_all(): return lax.all_to_all(copies, axis, split_axis=0, concat_axis=0, tiled=True)  36.6 us
    all_to_all x4, starting transfers between devices, sent_to_all(): return lax.all_to_all(copies, axis, split_axis=0, concat_axis=0, tiled=True)  28.4 us
    all_to_all x1, blocking collectives, sent_to_all(): return lax.all_to_all(copies, axis, split_axis=0, concat_axis=0, tiled=True)  28.4 us
    all_gather x2, waiting for transfers between devices, gather_in_order(): blocks = lax.all_gather(blocks, axes[k])  28 us
    all_to_all x3, starting transfers between devices, summed_on_arrival(): blocks = lax.all_to_all(split_up(array, dim, count), axis, 0, 0, tiled=True)  18.3 us
  transfers between devices with their start and end apart: 11, of which 9 were waited for; matrix products, arithmetic and copies ran while one was open for 4% of the time, Pallas kernels for 0%

commit v1 on v0

v1 whole, which is shorter than its diff:
```python
import functools

import jax
import jax.numpy as jnp
from jax import lax
from jax.experimental import pallas as pl
from jax.experimental.pallas import tpu as pltpu
from jax.sharding import PartitionSpec as P

MESH = pl.DeviceIdType.MESH
F32 = jnp.float32
BF16 = jnp.bfloat16
SUBS = 2


def dot(a, b, ca, cb):
    return lax.dot_general(a, b, (((ca,), (cb,)), ((), ())), preferred_element_type=F32)


def aligned(i, n):
    return pl.multiple_of(i * n, n)


def kernel(
    n_gx, n_gy, d_model,
    patches, gain, upstream, w_in, w_out, row_in, row_out,
    output, input_grad, grad_in, grad_out, vec_f, vec_c, totals,
    up_all, nrm_all, wo_p, wi_p, hg_part, pre_part, hg_u, hg_d, pr_u, pr_d, full,
    unit_s, stat_m, stat_p, stat_z, br, ng, br_in, ng_in, ph1, ph1_in, fin_m, fin_p, fin_z,
    col_m, col_p, col_h, col_z, col_o,
    up_ss, up_rs, nr_ss, nr_rs, pt_ss, pt_rs, st_ss, st_rs, fi_ss, fi_rs, co_ss, co_rs,
    hu_ss, hu_rs, hd_ss, hd_rs, pu_ss, pu_rs, pd_ss, pd_rs,
    gu_ss, gu_rs, gd_ss, gd_rs, gp_ss, gp_rs, br_ss, br_rs, ng_ss, ng_rs, p1_ss, p1_rs,
):
    gx = lax.axis_index("gx")
    gy = lax.axis_index("gy")
    nz = n_gx // 2
    z = lax.div(gx, 2)
    core = lax.rem(gx, 2)
    other = 1 - core
    lin = gy * 2 + core
    n_lin = 2 * n_gy
    block, feats = patches.shape
    rows = block * n_gy
    cols = w_in.shape[1]
    half = cols // 2
    share = rows // nz
    ups, downs = nz // 2, nz - 1 - nz // 2

    def zdev(zz):
        return {"gx": zz * 2 + core, "gy": gy}

    partner = {"gx": z * 2 + other, "gy": gy}
    z_up = lax.rem(z + 1, nz)
    z_down = lax.rem(z + nz - 1, nz)

    def lindev(p):
        return {"gx": z * 2 + lax.rem(p, 2), "gy": lax.div(p, 2)}

    def remote(src, dst, ss, rs, dev):
        return pltpu.make_async_remote_copy(
            src_ref=src, dst_ref=dst, send_sem=ss, recv_sem=rs, device_id=dev, device_id_type=MESH
        )

    def each(lo, hi, f):
        def step(j, carry):
            f(j)
            return carry
        if lo < hi:
            lax.fori_loop(lo, hi, step, 0)

    barrier = pltpu.get_barrier_semaphore()

    def greet(dev):
        pl.semaphore_signal(barrier, inc=1, device_id=dev, device_id_type=MESH)

    each(1, nz, lambda j: greet(zdev(lax.rem(z + j, nz))))
    each(1, n_lin, lambda j: greet(lindev(lax.rem(lin + j, n_lin))))
    pl.semaphore_wait(barrier, nz - 1 + n_lin - 1)

    def plane_start(src, everything, ss, rs):
        def go(j):
            p = lax.rem(lin + j, n_lin)
            remote(src, everything.at[core, pl.ds(aligned(gy, block), block)], ss.at[j], rs.at[lin], lindev(p)).start()
        each(1, n_lin, go)

    def plane_wait(src, everything, ss, rs):
        def done(j):
            p = lax.rem(lin + j, n_lin)
            landed = everything.at[lax.rem(p, 2), pl.ds(aligned(lax.div(p, 2), block), block)]
            copy = remote(src, landed, ss.at[j], rs.at[p], lindev(p))
            copy.wait_send()
            copy.wait_recv()
        each(1, n_lin, done)

    def chips_start(src, slots, ss, rs):
        def go(j):
            zz = lax.rem(z + j, nz)
            remote(src, slots.at[z], ss.at[j], rs.at[z], zdev(zz)).start()
        each(1, nz, go)

    def chips_wait(src, slots, ss, rs):
        def done(j):
            zz = lax.rem(z + j, nz)
            copy = remote(src, slots.at[zz], ss.at[j], rs.at[zz], zdev(zz))
            copy.wait_send()
            copy.wait_recv()
        each(1, nz, done)

    def scatter_start(src, slots, ss, rs, whole):
        def go(j):
            g = lax.rem(gy + j, n_gy)
            part = src if whole else src.at[pl.ds(aligned(g, block), block)]
            remote(part, slots.at[gy], ss.at[j], rs.at[gy], {"gx": gx, "gy": g}).start()
        each(1, n_gy, go)

    def scatter_wait(src, slots, ss, rs, whole):
        def done(j):
            g = lax.rem(gy + j, n_gy)
            part = src if whole else src.at[pl.ds(aligned(g, block), block)]
            copy = remote(part, slots.at[g], ss.at[j], rs.at[g], {"gx": gx, "gy": g})
            copy.wait_send()
            copy.wait_recv()
        each(1, n_gy, done)

    def to_partner(src, dst, k):
        return remote(src, dst, pt_ss.at[k], pt_rs.at[k], partner)

    def across(first, second):
        lane = lax.broadcasted_iota(jnp.int32, (block, 128), 1)
        tile = jnp.where(lane == 0, first, jnp.where(lane == 1, second, 0.0))
        if block < 128:
            tile = jnp.concatenate([tile, jnp.zeros((128 - block, 128), F32)], axis=0)
        return jnp.transpose(tile)[:8]

    def back(message):
        tile = jnp.concatenate([message, jnp.zeros((120, 128), F32)], axis=0)
        tile = jnp.transpose(tile)
        return tile[:block, 0:1], tile[:block, 1:2]

    plane_start(upstream, up_all, up_ss, up_rs)
    send_wo = to_partner(w_out.at[pl.ds(aligned(other, half), half)], wo_p, 0)
    send_wo.start()
    send_wi = to_partner(w_in.at[:, pl.ds(aligned(other, half), half)], wi_p, 1)
    send_wi.start()
    x_float = patches[...].astype(F32)
    stat_m[...] = across(
        jnp.sum(x_float, axis=1, keepdims=True), jnp.sum(x_float * x_float, axis=1, keepdims=True)
    )
    send_st = to_partner(stat_m, stat_p, 2)
    send_st.start()
    up_all[core, pl.ds(aligned(gy, block), block), :] = upstream[...]
    send_st.wait()
    stat_z[z] = stat_m[...] + stat_p[...]
    chips_start(stat_z.at[z], stat_z, st_ss, st_rs)

    tile = 128 if rows % 128 == 0 else rows

    plane_wait(upstream, up_all, up_ss, up_rs)
    send_wo.wait()

    def hg_tile(i):
        r = pl.ds(aligned(i, tile), tile)
        mine = dot(up_all[core, r, :], w_out[pl.ds(aligned(core, half), half), :], 1, 1)
        hg_part[r, :] = mine + dot(up_all[other, r, :], wo_p[...], 1, 1)
    each(0, rows // tile, hg_tile)

    piece = share // SUBS

    def ring_step(s, part, buf, ss, rs, target, neighbour, first):
        for sub in range(SUBS):
            at = pl.ds(sub * piece, piece)
            own = part[pl.ds(pl.multiple_of(target * share + sub * piece, piece), piece), :]
            here = buf.at[s, at]
            there = buf.at[s + 1, at]
            copy = remote(here, there, ss.at[s, sub], rs.at[s + 1, sub], neighbour)
            if first:
                buf[s, at, :] = own.astype(BF16)
            else:
                remote(here, here, ss.at[s, sub], rs.at[s, sub], neighbour).wait_recv()
                buf[s, at, :] = (buf[s, at, :].astype(F32) + own).astype(BF16)
            copy.start()

    def reduce_step(kind, s, up=True, down=True, first=False):
        part, bu, bd, uss, urs, dss, drs = kind
        if up:
            ring_step(s, part, bu, uss, urs, lax.rem(z + ups - s + nz, nz), zdev(z_up), first)
        if down:
            ring_step(s, part, bd, dss, drs, lax.rem(z + nz - downs + s, nz), zdev(z_down), first)

    def reduce_end(kind):
        part, bu, bd, uss, urs, dss, drs = kind
        for sub in range(SUBS):
            at = pl.ds(sub * piece, piece)
            remote(bu.at[ups, at], bu.at[ups, at], uss.at[0, sub], urs.at[ups, sub], zdev(z_up)).wait_recv()
            remote(bd.at[downs, at], bd.at[downs, at], dss.at[0, sub], drs.at[downs, sub], zdev(z_down)).wait_recv()
        own = part[pl.ds(aligned(z, share), share), :]
        return (own + bu[ups].astype(F32)) + bd[downs].astype(F32)

    def reduce_sent(kind):
        part, bu, bd, uss, urs, dss, drs = kind

        def sent(buf, ss, rs, neighbour):
            def one(s):
                for sub in range(SUBS):
                    here = buf.at[s, pl.ds(sub * piece, piece)]
                    remote(here, here, ss.at[s, sub], rs.at[s, sub], neighbour).wait_send()
            return one
        each(0, ups, sent(bu, uss, urs, zdev(z_up)))
        each(0, downs, sent(bd, dss, drs, zdev(z_down)))

    hg = (hg_part, hg_u, hg_d, hu_ss, hu_rs, hd_ss, hd_rs)
    pre = (pre_part, pr_u, pr_d, pu_ss, pu_rs, pd_ss, pd_rs)
    reduce_step(hg, 0, first=True)

    chips_wait(stat_z.at[z], stat_z, st_ss, st_rs)
    total, squares = back(jnp.sum(stat_z[...], axis=0))
    row_mean = total / d_model
    row_var = squares / d_model - row_mean * row_mean
    inv_std = lax.rsqrt(row_var + 1e-06)
    unit = (patches[...].astype(F32) - row_mean) * inv_std
    unit_s[...] = unit
    mine = pl.ds(aligned(gy, block), block)
    nrm_all[core, mine, :] = (unit * gain[...]).astype(BF16)
    plane_start(nrm_all.at[core, mine], nrm_all, nr_ss, nr_rs)

    lag = min(2, downs)
    each(1, lag, lambda s: reduce_step(hg, s))
    plane_wait(nrm_all.at[core, mine], nrm_all, nr_ss, nr_rs)
    send_wi.wait()

    def pre_tile(i):
        r = pl.ds(aligned(i, tile), tile)
        own = dot(nrm_all[core, r, :], w_in[:, pl.ds(aligned(core, half), half)], 1, 0)
        pre_part[r, :] = own + dot(nrm_all[other, r, :], wi_p[...], 1, 0)
    each(0, rows // tile, pre_tile)
    reduce_step(pre, 0, first=True)
    joint = downs - lag

    def both(i):
        reduce_step(hg, lag + i)
        reduce_step(pre, 1 + i)
    each(0, joint, both)
    if ups > downs:
        reduce_step(hg, ups - 1, down=False)
    each(1 + joint, downs, lambda s: reduce_step(pre, s))
    if ups > downs:
        reduce_step(pre, ups - 1, down=False)

    hidden_grad = reduce_end(hg).astype(BF16).astype(F32)
    hidden_pre = reduce_end(pre).astype(BF16).astype(F32)
    phi = 0.5 * (1.0 + lax.erf(hidden_pre * 0.7071067811865476))
    slope = phi + hidden_pre * jnp.exp(-0.5 * hidden_pre * hidden_pre) * 0.3989422804014327
    own_rows = pl.ds(aligned(z, share), share)
    full[0, core, own_rows, :] = (hidden_pre * phi).astype(BF16)
    full[1, core, own_rows, :] = (hidden_grad * slope).astype(BF16)

    def rows_of(origin):
        return pl.ds(aligned(origin, share), share)

    def spread(k, origin, ss, rs, neighbour):
        ref = full.at[k, core, rows_of(origin)]
        return remote(ref, ref, ss, rs, neighbour)

    def hand_over(k, origin):
        return spread(k, origin, gp_ss.at[origin, k], gp_rs.at[origin, k], partner)

    def gather_up(s, k):
        return spread(k, lax.rem(z - s + nz, nz), gu_ss.at[s, k], gu_rs.at[s + 1, k], zdev(z_up))

    def gather_down(s, k):
        return spread(k, lax.rem(z + s, nz), gd_ss.at[s, k], gd_rs.at[s + 1, k], zdev(z_down))

    def gather_step(s, wait_up=True, wait_down=True, send_up=True, send_down=True):
        for k in range(2):
            if wait_up:
                origin = lax.rem(z - s + nz, nz)
                spread(k, origin, gu_ss.at[0, k], gu_rs.at[s, k], zdev(z_up)).wait_recv()
                if send_up:
                    gather_up(s, k).start()
                hand_over(k, origin).start()
            if wait_down:
                origin = lax.rem(z + s, nz)
                spread(k, origin, gd_ss.at[0, k], gd_rs.at[s, k], zdev(z_down)).wait_recv()
                if send_down:
                    gather_down(s, k).start()
                hand_over(k, origin).start()

    for k in range(2):
        gather_up(0, k).start()
        gather_down(0, k).start()
        hand_over(k, z).start()
    each(1, downs, lambda s: gather_step(s))
    gather_step(downs, send_up=ups > downs, send_down=False)
    if ups > downs:
        gather_step(ups, wait_down=False, send_up=False)

    def handed(o):
        for k in range(2):
            ref = full.at[k, other, rows_of(o)]
            copy = remote(ref, ref, gp_ss.at[o, k], gp_rs.at[o, k], partner)
            copy.wait_send()
            copy.wait_recv()
    each(0, nz, handed)

    def branch_tile(i):
        r = pl.ds(aligned(i, tile), tile)
        out = dot(full[0, 0, r, :], w_out[:half, :], 1, 0) + dot(full[0, 1, r, :], w_out[half:, :], 1, 0)
        br[r, :] = out.astype(BF16)
    each(0, rows // tile, branch_tile)
    scatter_start(br, br_in, br_ss, br_rs, False)

    def normed_tile(i):
        r = pl.ds(aligned(i, tile), tile)
        out = dot(full[1, 0, r, :], w_in[:, :half], 1, 1) + dot(full[1, 1, r, :], w_in[:, half:], 1, 1)
        ng[r, :] = out.astype(BF16)
    each(0, rows // tile, normed_tile)
    scatter_start(ng, ng_in, ng_ss, ng_rs, False)

    def rough(values):
        high = values.astype(BF16)
        return high, (values - high.astype(F32)).astype(BF16)

    nrm_t = jnp.transpose(nrm_all[core])
    ones_f = jnp.ones((8, feats), BF16)
    row_in_sum = jnp.zeros((8, feats), F32)
    col_out_sum = jnp.zeros((1, feats), F32)
    lines = lax.broadcasted_iota(jnp.int32, (8, half // 2), 0)
    packed = jnp.zeros((8, half // 2), F32)
    for h in range(2):
        gi = dot(nrm_t, full[1, h], 1, 0)
        grad_in[:, h * half:(h + 1) * half] = gi
        sq = gi * gi + 1e-30
        high, low = rough(sq)
        ones_h = jnp.ones((8, half), BF16)
        row_in_sum += dot(ones_h, high, 1, 1) + dot(ones_h, low, 1, 1)
        col = jnp.sum(sq, axis=0, keepdims=True)
        for q in range(2):
            packed = jnp.where(lines == 2 * h + q, col[:, q * (half // 2):(q + 1) * (half // 2)], packed)
        go = dot(full[0, h], up_all[core], 0, 0)
        grad_out[h * half:(h + 1) * half, :] = go
        sq = go * go + 1e-30
        high, low = rough(sq)
        col_out_sum += jnp.sum(sq, axis=0, keepdims=True)
        row = dot(ones_f, high, 1, 1) + dot(ones_f, low, 1, 1)
        for q in range(2):
            packed = jnp.where(lines == 4 + 2 * h + q, row[:, q * (half // 2):(q + 1) * (half // 2)], packed)
    col_m[...] = packed
    send_col = to_partner(col_m, col_p, 3)
    send_col.start()
    eight = lax.broadcasted_iota(jnp.int32, (8, feats), 0)
    row_out_total = jnp.sum(row_out[...], axis=1, keepdims=True)
    ph1[...] = jnp.where(
        eight == 0, row_in_sum, jnp.where(eight == 1, col_out_sum, jnp.broadcast_to(row_out_total, (8, feats)))
    )
    scatter_start(ph1, ph1_in, p1_ss, p1_rs, True)

    send_col.wait()
    chip_cols = col_m[...] + col_p[...]
    col_h[...] = jnp.where(core == 0, chip_cols[:4], chip_cols[4:])
    chips_start(col_h, col_z, co_ss, co_rs)

    scatter_wait(br, br_in, br_ss, br_rs, False)
    br_in[gy] = br[mine, :]
    branch = jnp.sum(br_in[...].astype(F32), axis=0)
    output[...] = (patches[...].astype(F32) + branch).astype(BF16)
    scatter_wait(ng, ng_in, ng_ss, ng_rs, False)
    ng_in[gy] = ng[mine, :]
    scaled = jnp.sum(ng_in[...].astype(F32), axis=0) * gain[...]
    unit = unit_s[...]
    message = across(jnp.sum(scaled, axis=1, keepdims=True), jnp.sum(scaled * unit, axis=1, keepdims=True))
    scatter_wait(ph1, ph1_in, p1_ss, p1_rs, True)
    ph1_in[gy] = ph1[...]
    sums = jnp.sum(ph1_in[...], axis=0)
    vec_f[...] = sums
    row_new = 0.9 * row_in[...] + 0.1 * (sums[0:1] / cols_total(cols, n_gy))
    lane8 = lax.broadcasted_iota(jnp.int32, (8, 128), 0)
    total_in = jnp.sum(row_new, axis=1, keepdims=True)
    total_out = jnp.sum(sums[1:2], axis=1, keepdims=True)
    fin_m[...] = jnp.where(lane8 == 2, total_in, jnp.where(lane8 == 3, total_out, message))
    send_fin = to_partner(fin_m, fin_p, 4)
    send_fin.start()
    send_fin.wait()
    fin_z[z] = fin_m[...] + fin_p[...]
    chips_start(fin_z.at[z], fin_z, fi_ss, fi_rs)
    chips_wait(col_h, col_z, co_ss, co_rs)
    col_z[z] = col_h[...]
    col_o[core] = jnp.sum(col_z[...], axis=0)
    send_out = to_partner(col_o.at[core], col_o.at[core], 5)
    send_out.start()
    reduce_sent(hg)
    reduce_sent(pre)

    def gathered(s):
        for k in range(2):
            gather_up(s, k).wait_send()
    each(0, ups, gathered)

    def gathered_down(s):
        for k in range(2):
            gather_down(s, k).wait_send()
    each(0, downs, gathered_down)
    chips_wait(fin_z.at[z], fin_z, fi_ss, fi_rs)
    final = jnp.sum(fin_z[...], axis=0)
    first_sum, second_sum = back(final)
    inv_std = lax.rsqrt(row_var + 1e-06)
    input_grad[...] = upstream[...].astype(F32) + inv_std * (
        scaled - first_sum / d_model - unit * (second_sum / d_model)
    )
    totals[...] = final
    send_out.wait_send()
    remote(col_o.at[core], col_o.at[other], pt_ss.at[5], pt_rs.at[5], partner).wait_recv()
    vec_c[...] = col_o[...]


def cols_total(cols, n_gy):
    return cols * n_gy


def exchange(n_gx, n_gy, d_model, args):
    patches, gain, upstream, w_in, w_out, row_in, row_out = args
    block, feats = patches.shape
    cols = w_in.shape[1]
    rows, half, nz = block * n_gy, cols // 2, n_gx // 2
    share = rows // nz
    ups, downs = nz // 2, nz - 1 - nz // 2
    vmem = pl.BlockSpec(memory_space=pltpu.VMEM)
    sems = lambda *shape: pltpu.SemaphoreType.DMA(shape)
    quarter = half // 2
    shapes = [
        ((2, rows, feats), BF16), ((2, rows, feats), BF16), ((half, feats), BF16), ((feats, half), BF16),
        ((rows, half), F32), ((rows, half), F32),
        ((ups + 1, share, half), BF16), ((downs + 1, share, half), BF16),
        ((ups + 1, share, half), BF16), ((downs + 1, share, half), BF16),
        ((2, 2, rows, half), BF16),
        ((block, feats), F32), ((8, 128), F32), ((8, 128), F32), ((nz, 8, 128), F32),
        ((rows, feats), BF16), ((rows, feats), BF16), ((n_gy, block, feats), BF16), ((n_gy, block, feats), BF16),
        ((8, feats), F32), ((n_gy, 8, feats), F32),
        ((8, 128), F32), ((8, 128), F32), ((nz, 8, 128), F32),
        ((8, quarter), F32), ((8, quarter), F32), ((4, quarter), F32), ((nz, 4, quarter), F32), ((2, 4, quarter), F32),
    ]
    lin = 2 * n_gy
    semaphores = [
        sems(lin), sems(lin), sems(lin), sems(lin), sems(6), sems(6),
        sems(nz), sems(nz), sems(nz), sems(nz), sems(nz), sems(nz),
        sems(ups, SUBS), sems(ups + 1, SUBS), sems(downs, SUBS), sems(downs + 1, SUBS),
        sems(ups, SUBS), sems(ups + 1, SUBS), sems(downs, SUBS), sems(downs + 1, SUBS),
        sems(ups, 2), sems(ups + 1, 2), sems(downs, 2), sems(downs + 1, 2), sems(nz, 2), sems(nz, 2),
        sems(n_gy), sems(n_gy), sems(n_gy), sems(n_gy), sems(n_gy), sems(n_gy),
    ]
    outs = [
        jax.ShapeDtypeStruct((block, feats), BF16), jax.ShapeDtypeStruct((block, feats), F32),
        jax.ShapeDtypeStruct((feats, cols), F32), jax.ShapeDtypeStruct((cols, feats), F32),
        jax.ShapeDtypeStruct((8, feats), F32), jax.ShapeDtypeStruct((2, 4, quarter), F32),
        jax.ShapeDtypeStruct((8, 128), F32),
    ]
    return pl.pallas_call(
        functools.partial(kernel, n_gx, n_gy, d_model),
        out_shape=outs,
        in_specs=[vmem] * 7,
        out_specs=[vmem] * 7,
        scratch_shapes=[pltpu.VMEM(s, t) for s, t in shapes] + semaphores,
        compiler_params=pltpu.CompilerParams(
            collective_id=0, has_side_effects=True, vmem_limit_bytes=48 * 1024 * 1024
        ),
        name="block_step",
    )(*args)


def solution(mesh):
    n_gx, n_gy = mesh.shape["gx"], mesh.shape["gy"]

    def body(patches, ln_gain, weight_in, weight_out, upstream, row_in, col_in, row_out, col_out):
        feats, cols = weight_in.shape
        d_model, ff = feats * n_gx, cols * n_gy
        output, input_grad, grad_in, grad_out, vec_f, vec_c, totals = exchange(
            n_gx, n_gy, d_model,
            (patches, ln_gain[None], upstream, weight_in, weight_out, row_in[None], row_out[None]),
        )
        row_in_new = 0.9 * row_in + 0.1 * (vec_f[0] / ff)
        col_out_new = 0.9 * col_out + 0.1 * (vec_f[1] / ff)
        col_in_new = 0.9 * col_in + 0.1 * (vec_c[0].reshape(-1) / d_model)
        row_out_new = 0.9 * row_out + 0.1 * (vec_c[1].reshape(-1) / d_model)
        mean_in = totals[2, 0] / d_model
        mean_out = 0.9 * (vec_f[2, 0] / ff) + 0.1 * (totals[3, 0] / d_model / ff)
        update_in = grad_in / jnp.sqrt(row_in_new[:, None] * col_in_new[None, :] / mean_in)
        update_out = grad_out / jnp.sqrt(row_out_new[:, None] * col_out_new[None, :] / mean_out)
        return output, input_grad, update_in, update_out

    return jax.shard_map(
        body,
        mesh=mesh,
        in_specs=(
            P("gy", "gx"), P("gx"), P("gx", "gy"), P("gy", "gx"), P("gy", "gx"), P("gx"), P("gy"), P("gy"), P("gx"),
        ),
        out_specs=(P("gy", "gx"), P("gy", "gx"), P("gx", "gy"), P("gy", "gx")),
        check_vma=False,
    )
```

time: 406 us -> 137 us (0.34)
  waiting for transfers between devices: 168 us -> 0 us
  blocking collectives: 143 us -> 0 us
  Pallas kernels: 0 us -> 120 us
  starting transfers between devices: 46.8 us -> 0 us
  between operations: 16.7 us -> 2.63 us
  matrix products: 8.26 us -> 0 us
  other arithmetic: 8.25 us -> 3.7 us
    pallas_call x0 -> x1, Pallas kernels: none -> 120 us  [exchange(): pl.pallas_call(functools.partial(kernel, n_gx, n_gy, d_model), out_shape=...]
    reduce_scatter x2 -> x0, waiting for transfers between devices: 96.3 us -> none  [reduced_to_own(): blocks = lax.psum_scatter(blocks, axes[k], scatter_dimension=0, tiled=True)]
    psum x6 -> x0, blocking collectives: 59.7 us -> none  [over_axes(): return functools.reduce(lax.psum, axes, array)]
    all_gather x2 -> x0, blocking collectives: 54.8 us -> none  [gather_in_order(): blocks = lax.all_gather(blocks, axes[k])]
    all_to_all x7 -> x0, starting transfers between devices: 46.7 us -> none  [the longest x4 28.4 us: sent_to_all(): return lax.all_to_all(copies, axis, split_axis=0, concat_axis=0, tiled=True)]
    all_to_all x7 -> x0, waiting for transfers between devices: 43.6 us -> none  [the longest x4 36.6 us: sent_to_all(): return lax.all_to_all(copies, axis, split_axis=0, concat_axis=0, tiled=True)]
    all_to_all x1 -> x0, blocking collectives: 28.4 us -> none  [sent_to_all(): return lax.all_to_all(copies, axis, split_axis=0, concat_axis=0, tiled=True)]
    all_gather x2 -> x0, waiting for transfers between devices: 28 us -> none  [gather_in_order(): blocks = lax.all_gather(blocks, axes[k])]
  transfers between devices with their start and end apart: 11 -> 0, of which waited for: 9 -> 0; matrix products, arithmetic and copies ran while one was open for 4% -> 0% of each run, Pallas kernels for 0% -> 0%
where the time goes in v1:
time: 137 us; the launch traced here: 136 us
  Pallas kernels  120 us (88%)
  local copies, waits for them, and re-layouts  10.1 us (7%)
  other arithmetic  3.7 us (3%)
  between operations  2.63 us (2%)
    pallas_call x1, Pallas kernels, exchange(): pl.pallas_call(functools.partial(kernel, n_gx, n_gy, d_model), out_shape=...  120 us
    unnamed x30, local copies, waits for them, and re-layouts  8.41 us

profile of v1, /device:TPU:1, one launch (start us, length us, event | category | flops | bytes accessed | tf_op | source)
XLA Modules:
  0.0 136.2 jit_solution(10443961415596943308)
XLA Ops:
  0.6 0.0 copy-start.3
  0.6 0.0 copy-start.10
  0.7 1.3 copy.13.w_out
  2.0 0.0 copy-start
  2.0 1.1 copy-done
  3.1 0.7 copy-done.4
  3.8 0.7 copy-done.7
  4.5 0.7 copy-done.8
  5.2 119.7 %block_step.1 = (bf16[32,192]{1,0:T(8,128)(2,1)S(1)}, f32[32,192]{1,0:T(8,128)S(1)}, f32[192,1536]{1,0:T(8,128)S(1)}, f32[1536,192]{1,0:T(8,128)S(1)}, f32[8,192...) custom-call(bf16[32,192]{1,0:T(8,128)(2,1)S(1)} %copy-done.3, f32[1,192]{1,0:T(1,128)S(1)} %bitcast.7, ...), custom_call_target="tpu_custom_call" | custom-call | tf_op jit(solution)/shard_map/block_step/pallas_call | solution.py:457
  124.9 0.0 copy-start.1
  124.9 0.6 copy-done.1
  125.5 0.6 copy-done.5
  126.1 0.5 fusion
  127.4 0.7 multiply_add_fusion.1
  128.1 0.8 slice_multiply_fusion.2
  128.9 0.7 multiply_add_fusion.3
  129.5 1.2 rsqrt_multiply_fusion.1
  130.8 1.2 slice.26
  133.2 0.3 rsqrt_multiply_fusion
  133.5 0.0 copy-start.6
  133.5 0.0 copy-start.2
  133.5 1.5 %copy.14 = f32[1536,192]{0,1:T(8,128)} copy(f32[1536,192]{1,0:T(8,128)S(1)} %rsqrt_multiply_fusion) | data formatting | bytes 2359296
  135.0 0.6 copy.17
  135.6 0.6 copy.18
  (20 shorter events, 0.1 us)
Async XLA Ops:
  0.6 1.4 %copy-start.3 = (bf16[32,192]{1,0:T(8,128)(2,1)S(1)}, bf16[32,192]{1,0:T(8,128)(2,1)}, u32[]{:S(2)}) copy-start(bf16[32,192]{1,0:T(8,128)(2,1)} %patches.1) | copy-start | bytes 36868
  0.6 1.4 copy-start.10
  2.0 1.1 copy-start
  3.1 0.7 copy-start.4
  3.8 0.7 copy-start.7
  4.5 0.7 copy-start.8
  124.9 0.6 copy-start.1
  125.5 0.6 copy-start.5
  126.1 1.2 copy-start.9
  129.5 3.6 %copy-start.12 = (f32[192]{0:T(256)S(1)}, f32[192]{0:T(256)}, u32[]{:S(2)}) copy-start(f32[192]{0:T(256)} %param.17) | copy-start | bytes 2308
  129.5 3.6 %copy-start.11 = (f32[1536]{0:T(1024)S(1)}, f32[1536]{0:T(1024)}, u32[]{:S(2)}) copy-start(f32[1536]{0:T(1024)} %param.16) | copy-start | bytes 18436
  133.5 1.5 %copy-start.6 = (bf16[32,192]{1,0:T(8,128)(2,1)S(1)}, bf16[32,192]{1,0:T(8,128)(2,1)}, u32[]{:S(2)}) copy-start(bf16[32,192]{1,0:T(8,128)(2,1)} %copy-done.5) | copy-start | bytes 36868
  133.5 2.1 %copy-start.2 = (f32[32,192]{1,0:T(8,128)S(1)}, f32[32,192]{1,0:T(8,128)}, u32[]{:S(2)}) copy-start(f32[32,192]{1,0:T(8,128)} %copy-done.1) | copy-start | bytes 73732

commit v2 on v0

v2 whole, which is shorter than its diff:
```python
import functools

import jax
import jax.numpy as jnp
from jax import lax
from jax.experimental import pallas as pl
from jax.experimental.pallas import tpu as pltpu
from jax.sharding import PartitionSpec as P

MESH = pl.DeviceIdType.MESH
F32 = jnp.float32
BF16 = jnp.bfloat16
SUBS = 4
GSUBS = 2
LAG = 3


def dot(a, b, ca, cb):
    return lax.dot_general(a, b, (((ca,), (cb,)), ((), ())), preferred_element_type=F32)


def aligned(i, n):
    return pl.multiple_of(i * n, n)


def plane_offsets(n_gy):
    side = next(k for k in range(int(n_gy ** 0.5), 0, -1) if n_gy % k == 0)
    wide = n_gy // side

    def hops(dy, dx):
        return min(dy, side - dy) + min(dx, wide - dx)

    offsets = [(dy, dx) for dy in range(side) for dx in range(wide) if dy or dx]
    return side, wide, sorted(offsets, key=lambda o: hops(*o))


def kernel(
    n_gx, n_gy, d_model,
    patches_h, gain_h, upstream_h, w_in_h, w_out_h, row_in_h, col_out_h, col_in_h, row_out_h,
    output, input_grad, grad_in, grad_out, totals,
    patches, gain, upstream, w_in, w_out, row_in, col_out, col_in, row_out,
    up_all, x_all, nrm_all, wo_p, wi_p, gains, hg_part, pre_part, hg_buf, pre_buf, hg_x, pre_x, full,
    unit_s, stat_m, stat_p, stat_z, means, br, ng, br_in, ng_in, ph1, ph1_in, fin_z,
    col_m, col_p, col_h, col_z, col_o,
    ld, up_ss, up_rs, uf_ss, uf_rs, xs_ss, xs_rs, xf_ss, xf_rs, pt_ss, pt_rs, st_ss, st_rs, fi_ss, fi_rs, co_ss, co_rs,
    ms_ss, ms_rs, hr_ss, hr_rs, pr_ss, pr_rs, hx_ss, hx_rs, px_ss, px_rs,
    ga_ss, ga_rs, gp_ss, gp_rs, br_ss, br_rs, ng_ss, ng_rs, p1_ss, p1_rs,
):
    gx = lax.axis_index("gx")
    gy = lax.axis_index("gy")
    nz = n_gx // 2
    z = lax.div(gx, 2)
    core = lax.rem(gx, 2)
    other = 1 - core
    block, feats = patches.shape
    rows = block * n_gy
    cols = w_in.shape[1]
    ff = cols * n_gy
    half = cols // 2
    quarter = half // 2
    share = rows // nz
    far = nz // 2
    side, wide, offsets = plane_offsets(n_gy)
    gy_y, gy_x = lax.div(gy, wide), lax.rem(gy, wide)
    peers = [lax.rem(gy_y + dy, side) * wide + lax.rem(gy_x + dx, wide) for dy, dx in offsets]

    def zdev(zz):
        return {"gx": zz * 2 + core, "gy": gy}

    def pdev(g):
        return {"gx": gx, "gy": g}

    partner = {"gx": z * 2 + other, "gy": gy}
    turn = 1 - 2 * core

    def ahead(k):
        return lax.rem(z + turn * k + nz, nz)

    def behind(k):
        return lax.rem(z - turn * k + nz, nz)

    next_dev = zdev(ahead(1))

    def remote(src, dst, ss, rs, dev):
        return pltpu.make_async_remote_copy(
            src_ref=src, dst_ref=dst, send_sem=ss, recv_sem=rs, device_id=dev, device_id_type=MESH
        )

    def each(lo, hi, f):
        def step(j, carry):
            f(j)
            return carry
        if lo < hi:
            lax.fori_loop(lo, hi, step, 0)

    loads = [
        pltpu.make_async_copy(a, b, ld.at[k]) for k, (a, b) in enumerate((
            (upstream_h, upstream), (patches_h, patches), (w_out_h, w_out), (w_in_h, w_in),
            (gain_h, gain), (row_in_h, row_in), (col_out_h, col_out),
            (col_in_h, col_in), (row_out_h, row_out),
        ))
    ]
    for copy in loads:
        copy.start()

    barrier = pltpu.get_barrier_semaphore()

    def greet(dev):
        pl.semaphore_signal(barrier, inc=1, device_id=dev, device_id_type=MESH)

    each(1, n_gx, lambda j: greet({"gx": lax.rem(gx + j, n_gx), "gy": gy}))
    for g in peers:
        greet(pdev(g))
    x_float = None
    loads[1].wait()

    def across(first, second):
        lane = lax.broadcasted_iota(jnp.int32, (block, 128), 1)
        tile = jnp.where(lane == 0, first, jnp.where(lane == 1, second, 0.0))
        if block < 128:
            tile = jnp.concatenate([tile, jnp.zeros((128 - block, 128), F32)], axis=0)
        return jnp.transpose(tile)[:8]

    def back(message):
        tile = jnp.concatenate([message, jnp.zeros((128 - message.shape[0], 128), F32)], axis=0)
        tile = jnp.transpose(tile)
        return tile[:block, 0:1], tile[:block, 1:2]

    x_float = patches[...].astype(F32)
    stat_m[...] = across(
        jnp.sum(x_float, axis=1, keepdims=True), jnp.sum(x_float * x_float, axis=1, keepdims=True)
    )
    loads[0].wait()
    own_block = pl.ds(aligned(gy, block), block)
    up_all[core, own_block, :] = upstream[...]
    x_all[core, own_block, :] = patches[...]
    for copy in loads[2:]:
        copy.wait()
    gains[core] = gain[...]
    pl.semaphore_wait(barrier, n_gx - 1 + n_gy - 1)

    def to_partner(src, dst, k):
        return remote(src, dst, pt_ss.at[k], pt_rs.at[k], partner)

    def plane_start(src, everything, ss, rs, fs, fr):
        for k, g in enumerate(peers):
            remote(src, everything.at[core, own_block], ss.at[k], rs.at[gy], pdev(g)).start()
        remote(src, everything.at[core, own_block], fs.at[gy], fr.at[gy], partner).start()

    def plane_forward(src, everything, ss, rs, fs, fr):
        for k, g in enumerate(peers):
            landed = everything.at[core, pl.ds(aligned(g, block), block)]
            copy = remote(src, landed, ss.at[k], rs.at[g], pdev(g))
            copy.wait_recv()
            remote(landed, landed, fs.at[g], fr.at[g], partner).start()

    def plane_wait(src, everything, ss, rs, fs, fr):
        for k, g in enumerate(peers):
            remote(src, everything.at[core, own_block], ss.at[k], rs.at[g], pdev(g)).wait_send()

        def handed(g):
            landed = everything.at[other, pl.ds(aligned(g, block), block)]
            copy = remote(landed, landed, fs.at[g], fr.at[g], partner)
            copy.wait_send()
            copy.wait_recv()
        each(0, n_gy, handed)

    def chips_start(src, slots, ss, rs):
        def go(j):
            zz = lax.rem(z + j, nz)
            remote(src, slots.at[z], ss.at[j], rs.at[z], zdev(zz)).start()
        each(1, nz, go)

    def chips_wait(src, slots, ss, rs):
        def done(j):
            zz = lax.rem(z + j, nz)
            copy = remote(src, slots.at[zz], ss.at[j], rs.at[zz], zdev(zz))
            copy.wait_send()
            copy.wait_recv()
        each(1, nz, done)

    send_st = to_partner(stat_m, stat_p, 2)
    send_st.start()
    up = (upstream, up_all, up_ss, up_rs, uf_ss, uf_rs)
    plane_start(*up)
    send_wo = to_partner(w_out, wo_p, 0)
    send_wo.start()
    send_st.wait()
    stat_z[z] = stat_m[...] + stat_p[...]
    chips_start(stat_z.at[z], stat_z, st_ss, st_rs)
    xs = (patches, x_all, xs_ss, xs_rs, xf_ss, xf_rs)
    plane_start(*xs)
    send_wi = to_partner(w_in, wi_p, 1)
    send_wi.start()
    send_gain = to_partner(gains.at[core], gains.at[core], 5)
    send_gain.start()

    def rows_of(origin):
        return pl.ds(aligned(origin, share), share)

    def block_product(everything, own_weight, other_weight, t):
        r = rows_of(t)
        return dot(everything[core, r, :], own_weight, 1, 0) + dot(everything[other, r, :], other_weight, 1, 0)

    early = SUBS // 2
    strip_cols = cols // SUBS

    def sub_of(i):
        return lax.rem(i + core * early, SUBS)

    def prepare(kind, s):
        part, buf, ss, rs, everything, own_weight, other_weight, cross, xss, xrs = kind
        part[...] = block_product(everything, own_weight[...], other_weight[...], ahead(far - s))

    def reduce_step(kind, s):
        part, buf, ss, rs, everything, own_weight, other_weight, cross, xss, xrs = kind
        known = isinstance(s, int)
        for i in range(early if known and s == 0 else SUBS):
            sub = sub_of(i)
            own = part[:, pl.ds(pl.multiple_of(sub * strip_cols, 128), strip_cols)]
            here = buf.at[s, sub]
            if known and s == (0 if i < early else 1):
                buf[s, sub] = own.astype(BF16)
            else:
                remote(here, here, ss.at[s, sub], rs.at[s, sub], next_dev).wait_recv()
                buf[s, sub] = (buf[s, sub].astype(F32) + own).astype(BF16)
            remote(here, buf.at[s + 1, sub], ss.at[s, sub], rs.at[s + 1, sub], next_dev).start()

    def cross_copy(kind, i):
        part, buf, ss, rs, everything, own_weight, other_weight, cross, xss, xrs = kind
        return remote(buf.at[far, sub_of(early + i)], cross.at[i], xss.at[i], xrs.at[i], partner)

    def prepare_end(kind):
        part, buf, ss, rs, everything, own_weight, other_weight, cross, xss, xrs = kind
        mine = pl.ds(aligned(core, half), half)
        part[:, :half] = block_product(everything, own_weight[:, mine], other_weight[:, mine], z)

    def cross_start(kind):
        part, buf, ss, rs, everything, own_weight, other_weight, cross, xss, xrs = kind
        for i in range(early):
            sub = sub_of(early + i)
            remote(buf.at[far, sub], buf.at[far, sub], ss.at[0, sub], rs.at[far, sub], next_dev).wait_recv()
            cross_copy(kind, i).start()

    def reduce_end(kind, i):
        part, buf, ss, rs, everything, own_weight, other_weight, cross, xss, xrs = kind
        sub = sub_of(i)
        remote(buf.at[far, sub], buf.at[far, sub], ss.at[0, sub], rs.at[far, sub], next_dev).wait_recv()
        cross_copy(kind, i).wait_recv()
        own = part[:, i * strip_cols:(i + 1) * strip_cols]
        total = (own + buf[far, sub].astype(F32)) + cross[i].astype(F32)
        return total.astype(BF16).astype(F32)

    def reduce_sent(kind):
        part, buf, ss, rs, everything, own_weight, other_weight, cross, xss, xrs = kind

        def sent(s, count):
            for i in range(count):
                here = buf.at[s, sub_of(i)]
                remote(here, here, ss.at[s, sub_of(i)], rs.at[s, sub_of(i)], next_dev).wait_send()

        sent(0, early)
        each(1, far, lambda s: sent(s, SUBS))
        for i in range(early):
            cross_copy(kind, i).wait_send()

    hg = (hg_part, hg_buf, hr_ss, hr_rs, up_all, w_out, wo_p, hg_x, hx_ss, hx_rs)
    pre = (pre_part, pre_buf, pr_ss, pr_rs, nrm_all, w_in, wi_p, pre_x, px_ss, px_rs)

    plane_forward(*up)
    plane_wait(*up)
    send_wo.wait()
    prepare(hg, 0)
    reduce_step(hg, 0)
    prepare(hg, 1)

    chips_wait(stat_z.at[z], stat_z, st_ss, st_rs)
    stats = jnp.sum(stat_z[...], axis=0)
    row_mean = stats[0:1] / d_model
    row_var = stats[1:2] / d_model - row_mean * row_mean
    inv_row = lax.rsqrt(row_var + 1e-06)
    line8 = lax.broadcasted_iota(jnp.int32, (8, 128), 0)
    place = 2 * lax.rem(gy, 4)
    means[gy] = jnp.where(line8 == place, row_mean, jnp.where(line8 == place + 1, inv_row, 0.0))
    for k, g in enumerate(peers):
        remote(means.at[gy], means.at[gy], ms_ss.at[k], ms_rs.at[gy], pdev(g)).start()
    mean_own, inv_std = back(jnp.where(line8 == 0, row_mean, jnp.where(line8 == 1, inv_row, 0.0)))
    unit_s[...] = (patches[...].astype(F32) - mean_own) * inv_std
    plane_forward(*xs)
    reduce_step(hg, 1)
    lag = min(LAG, far)

    def hg_step(s):
        prepare(hg, s)
        reduce_step(hg, s)
    each(2, lag, hg_step)
    plane_wait(*xs)
    send_wi.wait()
    send_gain.wait_send()
    remote(gains.at[core], gains.at[other], pt_ss.at[5], pt_rs.at[5], partner).wait_recv()
    for k, g in enumerate(peers):
        copy = remote(means.at[gy], means.at[g], ms_ss.at[k], ms_rs.at[g], pdev(g))
        copy.wait_send()
        copy.wait_recv()
    tiles = [(means[4 * q] + means[4 * q + 1]) + (means[4 * q + 2] + means[4 * q + 3]) for q in range(n_gy // 4)]
    tiles.append(jnp.zeros((128 - 2 * n_gy, 128), F32))
    columns = jnp.transpose(jnp.concatenate(tiles, axis=0))
    for g in range(n_gy):
        r = slice(g * block, (g + 1) * block)
        for c in range(2):
            unit = (x_all[c, r, :].astype(F32) - columns[:block, 2 * g:2 * g + 1]) * columns[:block, 2 * g + 1:2 * g + 2]
            nrm_all[c, r, :] = (unit * gains[c]).astype(BF16)
    prepare(pre, 0)
    reduce_step(pre, 0)
    if lag < far:
        prepare(hg, lag)
    prepare(pre, 1)
    if lag < far:
        reduce_step(hg, lag)
    reduce_step(pre, 1)

    def both(i):
        prepare(hg, lag + 1 + i)
        prepare(pre, 2 + i)
        reduce_step(hg, lag + 1 + i)
        reduce_step(pre, 2 + i)
    joint = max(far - lag - 1, 0)
    each(0, joint, both)

    def pre_step(s):
        prepare(pre, s)
        reduce_step(pre, s)
    prepare_end(hg)
    cut_in = min(2 + joint, far - 1)
    each(2 + joint, far - 1, pre_step)
    if far - 1 >= 2 + joint:
        prepare(pre, far - 1)
        cross_start(hg)
        reduce_step(pre, far - 1)
    else:
        cross_start(hg)
    prepare_end(pre)
    cross_start(pre)
    for i in range(early):
        hidden_grad = reduce_end(hg, i)
        hidden_pre = reduce_end(pre, i)
        phi = 0.5 * (1.0 + lax.erf(hidden_pre * 0.7071067811865476))
        slope = phi + hidden_pre * jnp.exp(-0.5 * hidden_pre * hidden_pre) * 0.3989422804014327
        at = slice(i * strip_cols, (i + 1) * strip_cols)
        full[0, core, rows_of(z), at] = (hidden_pre * phi).astype(BF16)
        full[1, core, rows_of(z), at] = (hidden_grad * slope).astype(BF16)

    strip = share // GSUBS
    pieces = [(w, k, g) for w in range(2) for g in range(GSUBS) for k in range(2)]
    own_pieces, other_pieces = pieces[:len(pieces) // 2], pieces[len(pieces) // 2:]

    def spread(piece, origin, ss, rs, row, neighbour, to_row):
        w, k, g = piece
        h = core if w == 0 else other
        name = h * (2 * GSUBS) + g * 2 + k
        ref = full.at[k, h, pl.ds(pl.multiple_of(origin * share + g * strip, strip), strip)]
        return remote(ref, ref, ss.at[row, name], rs.at[to_row, name], neighbour)

    def ring_send(s, piece):
        return spread(piece, behind(s), ga_ss, ga_rs, s, next_dev, s + 1)

    def ring_arrival(s, piece):
        return spread(piece, behind(s), ga_ss, ga_rs, 0, next_dev, s)

    def hand_over(piece, origin):
        return spread(piece, origin, gp_ss, gp_rs, origin, partner, origin)

    def process(origins, first, awaited):
        def join(ref, *index):
            parts = [ref[(*index, rows_of(o), slice(None))] for o in origins]
            return parts[0] if len(parts) == 1 else jnp.concatenate(parts, axis=0)

        def arrive():
            for o, some in awaited:
                for piece in some:
                    hand_over(piece, o).wait_recv()

        def products(k):
            weight, out, slots, ss, rs = ((w_out, br, br_in, br_ss, br_rs), (w_in, ng, ng_in, ng_ss, ng_rs))[k]
            product = dot(join(full, k, 0), weight[:, :half], 1, 1) + dot(join(full, k, 1), weight[:, half:], 1, 1)
            product = product.astype(BF16)
            for i, o in enumerate(origins):
                out[rows_of(o), :] = product[i * share:(i + 1) * share]

                @pl.when(o != gy)
                def _():
                    remote(out.at[rows_of(o)], slots.at[gy], ss.at[o], rs.at[gy], pdev(o)).start()

        def gradient(k):
            left, grad = ((up_all, grad_out), (nrm_all, grad_in))[k]
            lhs = join(left, core)
            for h in range(2):
                at = slice(h * half, (h + 1) * half)
                term = dot(lhs, join(full, k, h), 0, 0)
                grad[:, at] = term if first else grad[:, at] + term

        def begin():
            arrive()
            products(0)

        return begin, lambda: products(1), lambda: gradient(0), lambda: gradient(1)

    def gather_step(s, forward, work):
        quarter_of = len(pieces) // 4
        for n, piece in enumerate(pieces):
            ring_arrival(s, piece).wait_recv()
            if piece in forward:
                ring_send(s, piece).start()
            hand_over(piece, behind(s)).start()
            if (n + 1) % quarter_of == 0:
                work[n // quarter_of]()

    for piece in own_pieces:
        ring_send(0, piece).start()
        hand_over(piece, z).start()
    for piece in other_pieces:
        hand_over(piece, z).wait_recv()
        ring_send(0, piece).start()

    def pair(s):
        return (behind(s), ahead(s)), False, ((ahead(s), pieces),)

    gather_step(1, pieces if far > 2 else own_pieces, process((z,), True, ()))
    if far > 2:
        each(2, far - 1, lambda s: gather_step(s, pieces, process(*pair(s - 1))))
        gather_step(far - 1, own_pieces, process(*pair(far - 2)))
    for work in process(*pair(far - 1)):
        work()
    for piece in own_pieces:
        ring_arrival(far, piece).wait_recv()
        hand_over(piece, behind(far)).start()
    for work in process((behind(far),), False, ((behind(far), other_pieces),)):
        work()

    def rough(values):
        high = values.astype(BF16)
        return high, (values - high.astype(F32)).astype(BF16)

    ones_h = jnp.ones((8, half), BF16)
    lines = lax.broadcasted_iota(jnp.int32, (8, quarter), 0)
    packed = jnp.zeros((8, quarter), F32)
    lane_sums = []
    for k, grad in enumerate((grad_in, grad_out)):
        lane_sum = jnp.zeros((8, feats), F32)
        for h in range(2):
            values = grad[:, h * half:(h + 1) * half]
            sq = values * values + 1e-30
            high, low = rough(sq)
            lane_sum += dot(ones_h, high, 1, 1) + dot(ones_h, low, 1, 1)
            col = jnp.sum(sq, axis=0, keepdims=True)
            for q in range(2):
                packed = jnp.where(lines == 4 * k + 2 * h + q, col[:, q * quarter:(q + 1) * quarter], packed)
        lane_sums.append(lane_sum)
    col_m[...] = packed
    send_col = to_partner(col_m, col_p, 3)
    send_col.start()
    eight = lax.broadcasted_iota(jnp.int32, (8, feats), 0)
    row_out_total = jnp.sum(jnp.sum(row_out[...], axis=0, keepdims=True), axis=1, keepdims=True)
    wide_feats = ph1.shape[1]
    message = jnp.where(
        eight == 0, lane_sums[0], jnp.where(eight == 1, lane_sums[1], jnp.broadcast_to(row_out_total, (8, feats)))
    )
    if wide_feats > feats:
        message = jnp.concatenate([message, jnp.zeros((8, wide_feats - feats), F32)], axis=1)
    ph1[...] = message
    for k, g in enumerate(peers):
        remote(ph1, ph1_in.at[gy], p1_ss.at[k], p1_rs.at[gy], pdev(g)).start()

    send_col.wait()
    chip_cols = col_m[...] + col_p[...]
    col_h[...] = jnp.where(core == 0, chip_cols[:4], chip_cols[4:])
    chips_start(col_h, col_z, co_ss, co_rs)

    def scattered(out, slots, ss, rs):
        for g in peers:
            copy = remote(out.at[rows_of(g)], slots.at[g], ss.at[g], rs.at[g], pdev(g))
            copy.wait_send()
            copy.wait_recv()
        slots[gy] = out[own_block, :]
        return jnp.sum(slots[...].astype(F32), axis=0)

    scaled = scattered(ng, ng_in, ng_ss, ng_rs) * gain[...]
    unit = unit_s[...]
    message = across(jnp.sum(scaled, axis=1, keepdims=True), jnp.sum(scaled * unit, axis=1, keepdims=True))[:4]
    for k, g in enumerate(peers):
        copy = remote(ph1, ph1_in.at[g], p1_ss.at[k], p1_rs.at[g], pdev(g))
        copy.wait_send()
        copy.wait_recv()
    ph1_in[gy] = ph1[...]
    sums = jnp.sum(ph1_in[...], axis=0)
    row_in_new = 0.9 * row_in[...] + 0.1 * (sums[0:1, :feats] / ff)
    col_out_new = 0.9 * col_out[...] + 0.1 * (sums[1:2, :feats] / ff)
    lane4 = lax.broadcasted_iota(jnp.int32, (4, 128), 0)
    total_in = jnp.sum(row_in_new, axis=1, keepdims=True)
    total_out = jnp.sum(sums[1:2, :feats], axis=1, keepdims=True)
    fin_z[gx] = jnp.where(lane4 == 2, total_in, jnp.where(lane4 == 3, total_out, message))

    def finish(j):
        return remote(fin_z.at[gx], fin_z.at[gx], fi_ss.at[j], fi_rs.at[gx], {"gx": lax.rem(gx + j, n_gx), "gy": gy})

    each(1, n_gx, lambda j: finish(j).start())
    output[...] = (patches[...].astype(F32) + scattered(br, br_in, br_ss, br_rs)).astype(BF16)

    pair = jnp.where(
        lax.broadcasted_iota(jnp.int32, (128, feats), 0) == 0, lax.rsqrt(row_in_new), lax.rsqrt(col_out_new)
    )
    if wide_feats > feats:
        pair = jnp.concatenate([pair, jnp.zeros((128, wide_feats - feats), F32)], axis=1)
    turned = [jnp.transpose(pair[:, i * 128:(i + 1) * 128]) for i in range(wide_feats // 128)]
    factors = (turned[0] if len(turned) == 1 else jnp.concatenate(turned, axis=0))[:feats]

    chips_wait(col_h, col_z, co_ss, co_rs)
    col_z[z] = col_h[...]
    col_o[core] = jnp.sum(col_z[...], axis=0)
    send_out = to_partner(col_o.at[core], col_o.at[core], 4)
    send_out.start()
    reduce_sent(hg)
    reduce_sent(pre)

    def ring_sent(s, some):
        for piece in some:
            ring_send(s, piece).wait_send()
    each(0, far - 1, lambda s: ring_sent(s, pieces))
    ring_sent(far - 1, own_pieces)

    def handed_over(o, some):
        for piece in some:
            hand_over(piece, o).wait_send()
    handed_over(z, own_pieces)
    each(1, far, lambda s: handed_over(behind(s), pieces))
    handed_over(behind(far), own_pieces)
    send_out.wait_send()
    remote(col_o.at[core], col_o.at[other], pt_ss.at[4], pt_rs.at[4], partner).wait_recv()
    lines = quarter // 128
    for k, (grad, before) in enumerate(((grad_in, col_in), (grad_out, row_out))):
        column_sums = col_o[k] / d_model
        for q in range(4):
            at = slice(q * quarter, (q + 1) * quarter)
            old = [before[q * lines + i:q * lines + i + 1, :] for i in range(lines)]
            old = old[0] if lines == 1 else jnp.concatenate(old, axis=1)
            column = lax.rsqrt(0.9 * old + 0.1 * column_sums[q:q + 1])
            grad[:, at] = grad[:, at] * (factors[:, k:k + 1] * column)

    def finished(j):
        copy = finish(j)
        copy.wait_send()
        source = lax.rem(gx + j, n_gx)
        remote(fin_z.at[gx], fin_z.at[source], fi_ss.at[j], fi_rs.at[source], {"gx": source, "gy": gy}).wait_recv()
    each(1, n_gx, finished)
    final = jnp.sum(fin_z[...], axis=0)
    first_sum, second_sum = back(final)
    input_grad[...] = upstream[...].astype(F32) + inv_std * (
        scaled - first_sum / d_model - unit * (second_sum / d_model)
    )
    mean_in = final[2:3] / d_model
    mean_out = 0.9 * (sums[2:3, :128] / ff) + 0.1 * (final[3:4] / d_model / ff)
    which = lax.broadcasted_iota(jnp.int32, (8, 128), 0)
    totals[...] = jnp.sqrt(jnp.where(which == 0, mean_in, mean_out))


def exchange(n_gx, n_gy, d_model, args):
    patches, gain, upstream, w_in, w_out, row_in, col_out, col_in, row_out = args
    block, feats = patches.shape
    cols = w_in.shape[1]
    rows, half, nz = block * n_gy, cols // 2, n_gx // 2
    share, far = rows // nz, nz // 2
    quarter = half // 2
    wide_feats = -(-feats // 128) * 128
    pieces = 4 * GSUBS
    strips = cols // SUBS
    early = SUBS // 2
    vmem = pl.BlockSpec(memory_space=pltpu.VMEM)
    hbm = pl.BlockSpec(memory_space=pltpu.HBM)
    shapes = [(a.shape, a.dtype) for a in args] + [
        ((2, rows, feats), BF16), ((2, rows, feats), BF16), ((2, rows, feats), BF16),
        ((feats, cols), BF16), ((feats, cols), BF16), ((2, 1, feats), F32),
        ((share, cols), F32), ((share, cols), F32),
        ((far + 1, SUBS, share, strips), BF16), ((far + 1, SUBS, share, strips), BF16),
        ((early, share, strips), BF16), ((early, share, strips), BF16),
        ((2, 2, rows, half), BF16),
        ((block, feats), F32), ((8, 128), F32), ((8, 128), F32), ((nz, 8, 128), F32), ((n_gy, 8, 128), F32),
        ((rows, feats), BF16), ((rows, feats), BF16), ((n_gy, block, feats), BF16), ((n_gy, block, feats), BF16),
        ((8, wide_feats), F32), ((n_gy, 8, wide_feats), F32), ((n_gx, 4, 128), F32),
        ((8, quarter), F32), ((8, quarter), F32), ((4, quarter), F32), ((nz, 4, quarter), F32), ((2, 4, quarter), F32),
    ]
    counts = [(9,)] + [(n_gy,)] * 8 + [(6,)] * 2 + [(nz,)] * 2 + [(n_gx,)] * 2 + [(nz,)] * 2
    counts += [(n_gy,)] * 2 + [(far, SUBS), (far + 1, SUBS)] * 2 + [(early,)] * 4
    counts += [(far, pieces), (far + 1, pieces)] + [(nz, pieces)] * 2 + [(n_gy,)] * 6
    outs = [
        jax.ShapeDtypeStruct((block, feats), BF16), jax.ShapeDtypeStruct((block, feats), F32),
        jax.ShapeDtypeStruct((feats, cols), F32), jax.ShapeDtypeStruct((feats, cols), F32),
        jax.ShapeDtypeStruct((8, 128), F32),
    ]
    return pl.pallas_call(
        functools.partial(kernel, n_gx, n_gy, d_model),
        out_shape=outs,
        in_specs=[hbm] * 9,
        out_specs=[vmem] * 5,
        scratch_shapes=[pltpu.VMEM(s, t) for s, t in shapes] + [pltpu.SemaphoreType.DMA(c) for c in counts],
        compiler_params=pltpu.CompilerParams(
            collective_id=0, has_side_effects=True, vmem_limit_bytes=48 * 1024 * 1024
        ),
        name="block_step",
    )(*(pltpu.with_memory_space_constraint(a, pltpu.HBM) for a in args))


def finish_kernel(
    output, input_grad, grad_in, grad_out, totals, output_h, input_grad_h, update_in_h, update_out_h, new_in, new_out, sems
):
    small = [
        pltpu.make_async_copy(output, output_h, sems.at[0]), pltpu.make_async_copy(input_grad, input_grad_h, sems.at[1])
    ]
    for copy in small:
        copy.start()
    half = grad_in.shape[1] // 2
    copies = []
    for k, (grad, new, target) in enumerate(((grad_in, new_in, update_in_h), (grad_out, new_out, update_out_h))):
        for h in range(2):
            at = slice(h * half, (h + 1) * half)
            new[:, at] = grad[:, at] * totals[k:k + 1, 0:1]
            part = pl.ds(h * half, half)
            copy = pltpu.make_async_copy(new.at[:, part], target.at[:, part], sems.at[2 + 2 * k + h])
            copy.start()
            copies.append(copy)
    for copy in small + copies:
        copy.wait()


def finish(output, input_grad, grad_in, grad_out, totals):
    vmem = pl.BlockSpec(memory_space=pltpu.VMEM)
    hbm = pl.BlockSpec(memory_space=pltpu.HBM)
    arrays = (output, input_grad, grad_in, grad_out)
    return pl.pallas_call(
        finish_kernel,
        out_shape=[jax.ShapeDtypeStruct(a.shape, a.dtype) for a in arrays],
        in_specs=[vmem] * 5,
        out_specs=[hbm] * 4,
        scratch_shapes=[
            pltpu.VMEM(grad_in.shape, F32), pltpu.VMEM(grad_out.shape, F32), pltpu.SemaphoreType.DMA((6,))
        ],
        compiler_params=pltpu.CompilerParams(vmem_limit_bytes=16 * 1024 * 1024),
        name="scale_updates",
    )(*arrays, totals)


def solution(mesh):
    n_gx, n_gy = mesh.shape["gx"], mesh.shape["gy"]

    def body(patches, ln_gain, weight_in, weight_out, upstream, row_in, col_in, row_out, col_out):
        d_model = weight_in.shape[0] * n_gx
        results = exchange(
            n_gx, n_gy, d_model,
            (
                patches, ln_gain[None], upstream, weight_in, weight_out.T, row_in[None], col_out[None],
                col_in.reshape(-1, 128), row_out.reshape(-1, 128),
            ),
        )
        output, input_grad, update_in, update_out = finish(*results)
        return output, input_grad, update_in, update_out.T

    return jax.shard_map(
        body,
        mesh=mesh,
        in_specs=(
            P("gy", "gx"), P("gx"), P("gx", "gy"), P("gy", "gx"), P("gy", "gx"), P("gx"), P("gy"), P("gy"), P("gx"),
        ),
        out_specs=(P("gy", "gx"), P("gy", "gx"), P("gx", "gy"), P("gy", "gx")),
        check_vma=False,
    )
```

time: 406 us -> 114 us (0.28); the launches traced: 402 us -> 114 us
  waiting for transfers between devices: 168 us -> 0 us
  blocking collectives: 143 us -> 0 us
  Pallas kernels: 0 us -> 113 us
  starting transfers between devices: 46.8 us -> 0 us
  between operations: 16.7 us -> 0.64 us
  local copies, waits for them, and re-layouts: 10.7 us -> 0 us
  matrix products: 8.26 us -> 0 us
  other arithmetic: 8.25 us -> 0 us
    pallas_call x0 -> x2, Pallas kernels: none -> 113 us  [the longest x1 112 us: exchange(): pl.pallas_call(functools.partial(kernel, n_gx, n_gy, d_model), out_shape=...]
    reduce_scatter x2 -> x0, waiting for transfers between devices: 96.3 us -> none  [reduced_to_own(): blocks = lax.psum_scatter(blocks, axes[k], scatter_dimension=0, tiled=True)]
    psum x6 -> x0, blocking collectives: 59.7 us -> none  [over_axes(): return functools.reduce(lax.psum, axes, array)]
    all_gather x2 -> x0, blocking collectives: 54.8 us -> none  [gather_in_order(): blocks = lax.all_gather(blocks, axes[k])]
    all_to_all x7 -> x0, starting transfers between devices: 46.7 us -> none  [the longest x4 28.4 us: sent_to_all(): return lax.all_to_all(copies, axis, split_axis=0, concat_axis=0, tiled=True)]
    all_to_all x7 -> x0, waiting for transfers between devices: 43.6 us -> none  [the longest x4 36.6 us: sent_to_all(): return lax.all_to_all(copies, axis, split_axis=0, concat_axis=0, tiled=True)]
    all_to_all x1 -> x0, blocking collectives: 28.4 us -> none  [sent_to_all(): return lax.all_to_all(copies, axis, split_axis=0, concat_axis=0, tiled=True)]
    all_gather x2 -> x0, waiting for transfers between devices: 28 us -> none  [gather_in_order(): blocks = lax.all_gather(blocks, axes[k])]
  transfers between devices with their start and end apart: 11 -> 0, of which waited for: 9 -> 0; matrix products, arithmetic and copies ran while one was open for 4% -> 0% of each run, Pallas kernels for 0% -> 0%
where the time goes in v2:
time: 114 us
  Pallas kernels  113 us (99%)
    pallas_call x1, Pallas kernels, exchange(): pl.pallas_call(functools.partial(kernel, n_gx, n_gy, d_model), out_shape=...  112 us

profile of v2, /device:TPU:1, one launch (start us, length us, event | category | flops | bytes accessed | tf_op | source)
XLA Modules:
  0.0 114.1 jit_solution(3462304356019526013)
XLA Ops:
  0.6 111.8 %block_step.1 = (bf16[32,192]{1,0:T(8,128)(2,1)S(1)}, f32[32,192]{1,0:T(8,128)S(1)}, f32[192,1536]{1,0:T(8,128)S(1)}, f32[192,1536]{1,0:T(8,128)S(1)}, f32[8,128]{1,0:T(8,128)S(1)}) custom-call(bf16[32,192]{1,0:T(8,128)(2,1)} %patches_h.1, f32[1,192]{1,0:T(1,128)} %bitcast.10, bf16[32,192]{1,0:T(8,128)(2,1)} %upstream_h.1, bf16[192,1536]{1,0:T(8,128)(2,1)} %w_in_h.1, ...), custom_call_target="tpu_custom_call" | custom-call | tf_op jit(solution)/shard_map/block_step/pallas_call | solution.py:599
  112.5 1.6 %scale_updates.1 = (bf16[32,192]{1,0:T(8,128)(2,1)}, f32[32,192]{1,0:T(8,128)}, f32[192,1536]{1,0:T(8,128)}, f32[192,1536]{1,0:T(8,128)}) custom-call(bf16[32,192]{1,0:T(8,128)(2,1)S(1)} %get-tuple-element.13.output, f32[32,192]{1,0:T(8,128)S(1)} %get-tuple-element.14.input_grad, f32[192,1536]{1,0:T(8,128)S(1)} %get-tuple-element.15.grad_in, ...), custom_call_target="tpu_custom_call" | custom-call | tf_op jit(solution)/shard_map/scale_updates/pallas_call | solution.py:638

commit v3 on v2

--- a/solution.py
+++ b/solution.py
@@ -12,7 +12,7 @@
 BF16 = jnp.bfloat16
 SUBS = 4
 GSUBS = 2
-LAG = 3
+LAG = 2
 
 
 def dot(a, b, ca, cb):
@@ -40,9 +40,9 @@
     output, input_grad, grad_in, grad_out, totals,
     patches, gain, upstream, w_in, w_out, row_in, col_out, col_in, row_out,
     up_all, x_all, nrm_all, wo_p, wi_p, gains, hg_part, pre_part, hg_buf, pre_buf, hg_x, pre_x, full,
-    unit_s, stat_m, stat_p, stat_z, means, br, ng, br_in, ng_in, ph1, ph1_in, fin_z,
+    unit_s, stat_z, means, br, ng, br_in, ng_in, ph1, ph1_in, fin_z, sum_z, sum_p,
     col_m, col_p, col_h, col_z, col_o,
-    ld, up_ss, up_rs, uf_ss, uf_rs, xs_ss, xs_rs, xf_ss, xf_rs, pt_ss, pt_rs, st_ss, st_rs, fi_ss, fi_rs, co_ss, co_rs,
+    ld, up_ss, up_rs, uf_ss, uf_rs, xs_ss, xs_rs, xf_ss, xf_rs, pt_ss, pt_rs, st_ss, st_rs, fi_ss, fi_rs, sz_ss, sz_rs, co_ss, co_rs, sp_ss, sp_rs,
     ms_ss, ms_rs, hr_ss, hr_rs, pr_ss, pr_rs, hx_ss, hx_rs, px_ss, px_rs,
     ga_ss, ga_rs, gp_ss, gp_rs, br_ss, br_rs, ng_ss, ng_rs, p1_ss, p1_rs,
 ):
@@ -116,18 +116,17 @@
 
     def across(first, second):
         lane = lax.broadcasted_iota(jnp.int32, (block, 128), 1)
-        tile = jnp.where(lane == 0, first, jnp.where(lane == 1, second, 0.0))
-        if block < 128:
-            tile = jnp.concatenate([tile, jnp.zeros((128 - block, 128), F32)], axis=0)
-        return jnp.transpose(tile)[:8]
+        parts = [jnp.where(lane == 0, first, 0.0), jnp.where(lane == 0, second, 0.0)]
+        if 2 * block < 128:
+            parts.append(jnp.zeros((128 - 2 * block, 128), F32))
+        return jnp.transpose(jnp.concatenate(parts, axis=0))[:1]
 
     def back(message):
-        tile = jnp.concatenate([message, jnp.zeros((128 - message.shape[0], 128), F32)], axis=0)
-        tile = jnp.transpose(tile)
-        return tile[:block, 0:1], tile[:block, 1:2]
+        tile = jnp.transpose(jnp.broadcast_to(message, (128, 128)))
+        return tile[:block, 0:1], tile[block:2 * block, 0:1]
 
     x_float = patches[...].astype(F32)
-    stat_m[...] = across(
+    stat_z[gx] = across(
         jnp.sum(x_float, axis=1, keepdims=True), jnp.sum(x_float * x_float, axis=1, keepdims=True)
     )
     loads[0].wait()
@@ -179,15 +178,38 @@
             copy.wait_recv()
         each(1, nz, done)
 
-    send_st = to_partner(stat_m, stat_p, 2)
-    send_st.start()
+    def column_copy(slots, ss, rs, j, source):
+        return remote(slots.at[gx], slots.at[source], ss.at[j], rs.at[source], {"gx": lax.rem(gx + j, n_gx), "gy": gy})
+
+    def column_start(slots, ss, rs):
+        each(1, n_gx, lambda j: column_copy(slots, ss, rs, j, gx).start())
+
+    def column_wait(slots, ss, rs):
+        def done(j):
+            copy = column_copy(slots, ss, rs, j, lax.rem(gx + j, n_gx))
+            copy.wait_send()
+            copy.wait_recv()
+        each(1, n_gx, done)
+
+    def small_copy(slots, ss, rs, k, source):
+        return remote(slots.at[gy], slots.at[source], ss.at[k], rs.at[source], pdev(peers[k]))
+
+    def small_start(slots, ss, rs):
+        for k in range(len(peers)):
+            small_copy(slots, ss, rs, k, gy).start()
+
+    def small_wait(slots, ss, rs):
+        for k, g in enumerate(peers):
+            copy = small_copy(slots, ss, rs, k, g)
+            copy.wait_send()
+            copy.wait_recv()
+
+    stat = (stat_z, st_ss, st_rs)
+    column_start(*stat)
     up = (upstream, up_all, up_ss, up_rs, uf_ss, uf_rs)
     plane_start(*up)
     send_wo = to_partner(w_out, wo_p, 0)
     send_wo.start()
-    send_st.wait()
-    stat_z[z] = stat_m[...] + stat_p[...]
-    chips_start(stat_z.at[z], stat_z, st_ss, st_rs)
     xs = (patches, x_all, xs_ss, xs_rs, xf_ss, xf_rs)
     plane_start(*xs)
     send_wi = to_partner(w_in, wi_p, 1)
@@ -268,24 +290,21 @@
     pre = (pre_part, pre_buf, pr_ss, pr_rs, nrm_all, w_in, wi_p, pre_x, px_ss, px_rs)
 
     plane_forward(*up)
+    column_wait(*stat)
+    total, squares = back(jnp.sum(stat_z[...], axis=0))
+    row_mean = total / d_model
+    row_var = squares / d_model - row_mean * row_mean
+    inv_std = lax.rsqrt(row_var + 1e-06)
+    means[gy] = across(row_mean, inv_std)
+    deviations = (means, ms_ss, ms_rs)
+    small_start(*deviations)
     plane_wait(*up)
     send_wo.wait()
     prepare(hg, 0)
     reduce_step(hg, 0)
     prepare(hg, 1)
 
-    chips_wait(stat_z.at[z], stat_z, st_ss, st_rs)
-    stats = jnp.sum(stat_z[...], axis=0)
-    row_mean = stats[0:1] / d_model
-    row_var = stats[1:2] / d_model - row_mean * row_mean
-    inv_row = lax.rsqrt(row_var + 1e-06)
-    line8 = lax.broadcasted_iota(jnp.int32, (8, 128), 0)
-    place = 2 * lax.rem(gy, 4)
-    means[gy] = jnp.where(line8 == place, row_mean, jnp.where(line8 == place + 1, inv_row, 0.0))
-    for k, g in enumerate(peers):
-        remote(means.at[gy], means.at[gy], ms_ss.at[k], ms_rs.at[gy], pdev(g)).start()
-    mean_own, inv_std = back(jnp.where(line8 == 0, row_mean, jnp.where(line8 == 1, inv_row, 0.0)))
-    unit_s[...] = (patches[...].astype(F32) - mean_own) * inv_std
+    unit_s[...] = (patches[...].astype(F32) - row_mean) * inv_std
     plane_forward(*xs)
     reduce_step(hg, 1)
     lag = min(LAG, far)
@@ -298,17 +317,16 @@
     send_wi.wait()
     send_gain.wait_send()
     remote(gains.at[core], gains.at[other], pt_ss.at[5], pt_rs.at[5], partner).wait_recv()
-    for k, g in enumerate(peers):
-        copy = remote(means.at[gy], means.at[g], ms_ss.at[k], ms_rs.at[g], pdev(g))
-        copy.wait_send()
-        copy.wait_recv()
-    tiles = [(means[4 * q] + means[4 * q + 1]) + (means[4 * q + 2] + means[4 * q + 3]) for q in range(n_gy // 4)]
-    tiles.append(jnp.zeros((128 - 2 * n_gy, 128), F32))
-    columns = jnp.transpose(jnp.concatenate(tiles, axis=0))
+    small_wait(*deviations)
+    lines = lax.broadcasted_iota(jnp.int32, (128, 128), 0)
+    columns = jnp.zeros((128, 128), F32)
+    for g in range(n_gy):
+        columns = jnp.where(lines == g, means[g], columns)
+    columns = jnp.transpose(columns)
     for g in range(n_gy):
         r = slice(g * block, (g + 1) * block)
         for c in range(2):
-            unit = (x_all[c, r, :].astype(F32) - columns[:block, 2 * g:2 * g + 1]) * columns[:block, 2 * g + 1:2 * g + 2]
+            unit = (x_all[c, r, :].astype(F32) - columns[:block, g:g + 1]) * columns[block:2 * block, g:g + 1]
             nrm_all[c, r, :] = (unit * gains[c]).astype(BF16)
     prepare(pre, 0)
     reduce_step(pre, 0)
@@ -406,14 +424,13 @@
         return begin, lambda: products(1), lambda: gradient(0), lambda: gradient(1)
 
     def gather_step(s, forward, work):
-        quarter_of = len(pieces) // 4
-        for n, piece in enumerate(pieces):
+        for piece in pieces:
             ring_arrival(s, piece).wait_recv()
             if piece in forward:
                 ring_send(s, piece).start()
             hand_over(piece, behind(s)).start()
-            if (n + 1) % quarter_of == 0:
-                work[n // quarter_of]()
+        for part in work:
+            part()
 
     for piece in own_pieces:
         ring_send(0, piece).start()
@@ -422,14 +439,17 @@
         hand_over(piece, z).wait_recv()
         ring_send(0, piece).start()
 
-    def pair(s):
-        return (behind(s), ahead(s)), False, ((ahead(s), pieces),)
-
-    gather_step(1, pieces if far > 2 else own_pieces, process((z,), True, ()))
-    if far > 2:
-        each(2, far - 1, lambda s: gather_step(s, pieces, process(*pair(s - 1))))
-        gather_step(far - 1, own_pieces, process(*pair(far - 2)))
-    for work in process(*pair(far - 1)):
+    def pairs(*steps):
+        origins = sum(((behind(s), ahead(s)) for s in steps), ())
+        return origins, False, tuple((ahead(s), pieces) for s in steps)
+
+    todo = list(process((z,), True, ()))
+    for s in range(1, far):
+        if s >= 3 and s % 2 == 1:
+            todo += process(*pairs(s - 2, s - 1))
+        gather_step(s, pieces if s < far - 1 else own_pieces, todo[:2] if s < far - 1 else todo)
+        todo = todo[2:] if s < far - 1 else []
+    for work in process(*pairs(*((far - 1,) if far % 2 == 0 else (far - 2, far - 1)))):
         work()
     for piece in own_pieces:
         ring_arrival(far, piece).wait_recv()
@@ -460,11 +480,19 @@
     send_col = to_partner(col_m, col_p, 3)
     send_col.start()
     eight = lax.broadcasted_iota(jnp.int32, (8, feats), 0)
-    row_out_total = jnp.sum(jnp.sum(row_out[...], axis=0, keepdims=True), axis=1, keepdims=True)
+    lane1 = lax.broadcasted_iota(jnp.int32, (1, 128), 1)
+
+    def total(values):
+        return jnp.sum(values, axis=1, keepdims=True)
+
+    def three(a, b, c):
+        return jnp.where(lane1 == 0, a, jnp.where(lane1 == 1, b, c))
+
+    sum_z[gx] = three(total(lane_sums[0][0:1]), total(lane_sums[1][0:1]), total(row_in[...]))
+    sums_z = (sum_z, sz_ss, sz_rs)
+    column_start(*sums_z)
     wide_feats = ph1.shape[1]
-    message = jnp.where(
-        eight == 0, lane_sums[0], jnp.where(eight == 1, lane_sums[1], jnp.broadcast_to(row_out_total, (8, feats)))
-    )
+    message = jnp.where(eight == 0, lane_sums[0], lane_sums[1])
     if wide_feats > feats:
         message = jnp.concatenate([message, jnp.zeros((8, wide_feats - feats), F32)], axis=1)
     ph1[...] = message
@@ -473,7 +501,7 @@
 
     send_col.wait()
     chip_cols = col_m[...] + col_p[...]
-    col_h[...] = jnp.where(core == 0, chip_cols[:4], chip_cols[4:])
+    col_h[...] = jnp.where(core == 0, chip_cols[:4], chip_cols[4:]).astype(BF16)
     chips_start(col_h, col_z, co_ss, co_rs)
 
     def scattered(out, slots, ss, rs):
@@ -486,7 +514,11 @@
 
     scaled = scattered(ng, ng_in, ng_ss, ng_rs) * gain[...]
     unit = unit_s[...]
-    message = across(jnp.sum(scaled, axis=1, keepdims=True), jnp.sum(scaled * unit, axis=1, keepdims=True))[:4]
+    message = across(jnp.sum(scaled, axis=1, keepdims=True), jnp.sum(scaled * unit, axis=1, keepdims=True))
+    fin_z[gx] = message
+    fin = (fin_z, fi_ss, fi_rs)
+    column_start(*fin)
+    output[...] = (patches[...].astype(F32) + scattered(br, br_in, br_ss, br_rs)).astype(BF16)
     for k, g in enumerate(peers):
         copy = remote(ph1, ph1_in.at[g], p1_ss.at[k], p1_rs.at[g], pdev(g))
         copy.wait_send()
@@ -495,16 +527,6 @@
     sums = jnp.sum(ph1_in[...], axis=0)
     row_in_new = 0.9 * row_in[...] + 0.1 * (sums[0:1, :feats] / ff)
     col_out_new = 0.9 * col_out[...] + 0.1 * (sums[1:2, :feats] / ff)
-    lane4 = lax.broadcasted_iota(jnp.int32, (4, 128), 0)
-    total_in = jnp.sum(row_in_new, axis=1, keepdims=True)
-    total_out = jnp.sum(sums[1:2, :feats], axis=1, keepdims=True)
-    fin_z[gx] = jnp.where(lane4 == 2, total_in, jnp.where(lane4 == 3, total_out, message))
-
-    def finish(j):
-        return remote(fin_z.at[gx], fin_z.at[gx], fi_ss.at[j], fi_rs.at[gx], {"gx": lax.rem(gx + j, n_gx), "gy": gy})
-
-    each(1, n_gx, lambda j: finish(j).start())
-    output[...] = (patches[...].astype(F32) + scattered(br, br_in, br_ss, br_rs)).astype(BF16)
 
     pair = jnp.where(
         lax.broadcasted_iota(jnp.int32, (128, feats), 0) == 0, lax.rsqrt(row_in_new), lax.rsqrt(col_out_new)
@@ -514,9 +536,15 @@
     turned = [jnp.transpose(pair[:, i * 128:(i + 1) * 128]) for i in range(wide_feats // 128)]
     factors = (turned[0] if len(turned) == 1 else jnp.concatenate(turned, axis=0))[:feats]
 
+    column_wait(*sums_z)
+    along = jnp.sum(sum_z[...], axis=0)
+    old_rows = along[:, 2:3]
+    sum_p[gy] = three(along[:, 0:1], along[:, 1:2], total(jnp.sum(row_out[...], axis=0, keepdims=True)))
+    sums_p = (sum_p, sp_ss, sp_rs)
+    small_start(*sums_p)
     chips_wait(col_h, col_z, co_ss, co_rs)
     col_z[z] = col_h[...]
-    col_o[core] = jnp.sum(col_z[...], axis=0)
+    col_o[core] = jnp.sum(col_z[...].astype(F32), axis=0)
     send_out = to_partner(col_o.at[core], col_o.at[core], 4)
     send_out.start()
     reduce_sent(hg)
@@ -546,19 +574,16 @@
             column = lax.rsqrt(0.9 * old + 0.1 * column_sums[q:q + 1])
             grad[:, at] = grad[:, at] * (factors[:, k:k + 1] * column)
 
-    def finished(j):
-        copy = finish(j)
-        copy.wait_send()
-        source = lax.rem(gx + j, n_gx)
-        remote(fin_z.at[gx], fin_z.at[source], fi_ss.at[j], fi_rs.at[source], {"gx": source, "gy": gy}).wait_recv()
-    each(1, n_gx, finished)
+    small_wait(*sums_p)
+    everything_sum = jnp.sum(sum_p[...], axis=0)
+    column_wait(*fin)
     final = jnp.sum(fin_z[...], axis=0)
     first_sum, second_sum = back(final)
     input_grad[...] = upstream[...].astype(F32) + inv_std * (
         scaled - first_sum / d_model - unit * (second_sum / d_model)
     )
-    mean_in = final[2:3] / d_model
-    mean_out = 0.9 * (sums[2:3, :128] / ff) + 0.1 * (final[3:4] / d_model / ff)
+    mean_in = (0.9 * old_rows + 0.1 * (everything_sum[:, 0:1] / ff)) / d_model
+    mean_out = (0.9 * everything_sum[:, 2:3] + 0.1 * (everything_sum[:, 1:2] / d_model)) / ff
     which = lax.broadcasted_iota(jnp.int32, (8, 128), 0)
     totals[...] = jnp.sqrt(jnp.where(which == 0, mean_in, mean_out))
 
@@ -583,12 +608,12 @@
         ((far + 1, SUBS, share, strips), BF16), ((far + 1, SUBS, share, strips), BF16),
         ((early, share, strips), BF16), ((early, share, strips), BF16),
         ((2, 2, rows, half), BF16),
-        ((block, feats), F32), ((8, 128), F32), ((8, 128), F32), ((nz, 8, 128), F32), ((n_gy, 8, 128), F32),
+        ((block, feats), F32), ((n_gx, 1, 128), F32), ((n_gy, 1, 128), F32),
         ((rows, feats), BF16), ((rows, feats), BF16), ((n_gy, block, feats), BF16), ((n_gy, block, feats), BF16),
-        ((8, wide_feats), F32), ((n_gy, 8, wide_feats), F32), ((n_gx, 4, 128), F32),
-        ((8, quarter), F32), ((8, quarter), F32), ((4, quarter), F32), ((nz, 4, quarter), F32), ((2, 4, quarter), F32),
+        ((8, wide_feats), F32), ((n_gy, 8, wide_feats), F32), ((n_gx, 1, 128), F32), ((n_gx, 1, 128), F32), ((n_gy, 1, 128), F32),
+        ((8, quarter), F32), ((8, quarter), F32), ((4, quarter), BF16), ((nz, 4, quarter), BF16), ((2, 4, quarter), F32),
     ]
-    counts = [(9,)] + [(n_gy,)] * 8 + [(6,)] * 2 + [(nz,)] * 2 + [(n_gx,)] * 2 + [(nz,)] * 2
+    counts = [(9,)] + [(n_gy,)] * 8 + [(6,)] * 2 + [(n_gx,)] * 6 + [(nz,)] * 2 + [(n_gy,)] * 2
     counts += [(n_gy,)] * 2 + [(far, SUBS), (far + 1, SUBS)] * 2 + [(early,)] * 4
     counts += [(far, pieces), (far + 1, pieces)] + [(nz, pieces)] * 2 + [(n_gy,)] * 6
     outs = [

time: 114 us -> 112 us (0.982)
  Pallas kernels: 113 us -> 111 us
    pallas_call x1, Pallas kernels: 112 us -> 110 us  [exchange(): pl.pallas_call(functools.partial(kernel, n_gx, n_gy, d_model), out_shape=...]
where the time goes in v3:
time: 112 us
  Pallas kernels  111 us (99%)
    pallas_call x1, Pallas kernels, exchange(): pl.pallas_call(functools.partial(kernel, n_gx, n_gy, d_model), out_shape=...  110 us

profile of v3, /device:TPU:1, one launch (start us, length us, event | category | flops | bytes accessed | tf_op | source)
XLA Modules:
  0.0 111.8 jit_solution(14372169510055059166)
XLA Ops:
  0.6 109.5 %block_step.1 = (bf16[32,192]{1,0:T(8,128)(2,1)S(1)}, f32[32,192]{1,0:T(8,128)S(1)}, f32[192,1536]{1,0:T(8,128)S(1)}, f32[192,1536]{1,0:T(8,128)S(1)}, f32[8,128]{1,0:T(8,128)S(1)}) custom-call(bf16[32,192]{1,0:T(8,128)(2,1)} %patches_h.1, f32[1,192]{1,0:T(1,128)} %bitcast.10, bf16[32,192]{1,0:T(8,128)(2,1)} %upstream_h.1, bf16[192,1536]{1,0:T(8,128)(2,1)} %w_in_h.1, ...), custom_call_target="tpu_custom_call" | custom-call | tf_op jit(solution)/shard_map/block_step/pallas_call | solution.py:624
  110.2 1.6 %scale_updates.1 = (bf16[32,192]{1,0:T(8,128)(2,1)}, f32[32,192]{1,0:T(8,128)}, f32[192,1536]{1,0:T(8,128)}, f32[192,1536]{1,0:T(8,128)}) custom-call(bf16[32,192]{1,0:T(8,128)(2,1)S(1)} %get-tuple-element.13.output, f32[32,192]{1,0:T(8,128)S(1)} %get-tuple-element.14.input_grad, f32[192,1536]{1,0:T(8,128)S(1)} %get-tuple-element.15.grad_in, ...), custom_call_target="tpu_custom_call" | custom-call | tf_op jit(solution)/shard_map/scale_updates/pallas_call | solution.py:663

commit v4 on v3

--- a/solution.py
+++ b/solution.py
@@ -289,7 +289,6 @@
     hg = (hg_part, hg_buf, hr_ss, hr_rs, up_all, w_out, wo_p, hg_x, hx_ss, hx_rs)
     pre = (pre_part, pre_buf, pr_ss, pr_rs, nrm_all, w_in, wi_p, pre_x, px_ss, px_rs)
 
-    plane_forward(*up)
     column_wait(*stat)
     total, squares = back(jnp.sum(stat_z[...], axis=0))
     row_mean = total / d_model
@@ -298,6 +297,7 @@
     means[gy] = across(row_mean, inv_std)
     deviations = (means, ms_ss, ms_rs)
     small_start(*deviations)
+    plane_forward(*up)
     plane_wait(*up)
     send_wo.wait()
     prepare(hg, 0)
@@ -461,36 +461,44 @@
         high = values.astype(BF16)
         return high, (values - high.astype(F32)).astype(BF16)
 
-    ones_h = jnp.ones((8, half), BF16)
+    def squares_of(k, h):
+        values = (grad_in, grad_out)[k][:, h * half:(h + 1) * half]
+        return values * values + 1e-30
+
+    lane1 = lax.broadcasted_iota(jnp.int32, (1, 128), 1)
+
+    def total(values):
+        return jnp.sum(values, axis=1, keepdims=True)
+
+    def three(a, b, c):
+        return jnp.where(lane1 == 0, a, jnp.where(lane1 == 1, b, c))
+
     lines = lax.broadcasted_iota(jnp.int32, (8, quarter), 0)
     packed = jnp.zeros((8, quarter), F32)
-    lane_sums = []
-    for k, grad in enumerate((grad_in, grad_out)):
-        lane_sum = jnp.zeros((8, feats), F32)
+    grand = []
+    for k in range(2):
+        grand.append(jnp.zeros((1, 1), F32))
         for h in range(2):
-            values = grad[:, h * half:(h + 1) * half]
-            sq = values * values + 1e-30
-            high, low = rough(sq)
-            lane_sum += dot(ones_h, high, 1, 1) + dot(ones_h, low, 1, 1)
-            col = jnp.sum(sq, axis=0, keepdims=True)
+            col = jnp.sum(squares_of(k, h), axis=0, keepdims=True)
+            grand[k] += total(col)
             for q in range(2):
                 packed = jnp.where(lines == 4 * k + 2 * h + q, col[:, q * quarter:(q + 1) * quarter], packed)
-        lane_sums.append(lane_sum)
+    sum_z[gx] = three(grand[0], grand[1], total(row_in[...]))
+    sums_z = (sum_z, sz_ss, sz_rs)
+    column_start(*sums_z)
     col_m[...] = packed
     send_col = to_partner(col_m, col_p, 3)
     send_col.start()
+
+    ones_h = jnp.ones((8, half), BF16)
+    lane_sums = []
+    for k in range(2):
+        lane_sum = jnp.zeros((8, feats), F32)
+        for h in range(2):
+            high, low = rough(squares_of(k, h))
+            lane_sum += dot(ones_h, high, 1, 1) + dot(ones_h, low, 1, 1)
+        lane_sums.append(lane_sum)
     eight = lax.broadcasted_iota(jnp.int32, (8, feats), 0)
-    lane1 = lax.broadcasted_iota(jnp.int32, (1, 128), 1)
-
-    def total(values):
-        return jnp.sum(values, axis=1, keepdims=True)
-
-    def three(a, b, c):
-        return jnp.where(lane1 == 0, a, jnp.where(lane1 == 1, b, c))
-
-    sum_z[gx] = three(total(lane_sums[0][0:1]), total(lane_sums[1][0:1]), total(row_in[...]))
-    sums_z = (sum_z, sz_ss, sz_rs)
-    column_start(*sums_z)
     wide_feats = ph1.shape[1]
     message = jnp.where(eight == 0, lane_sums[0], lane_sums[1])
     if wide_feats > feats:
@@ -519,6 +527,12 @@
     fin = (fin_z, fi_ss, fi_rs)
     column_start(*fin)
     output[...] = (patches[...].astype(F32) + scattered(br, br_in, br_ss, br_rs)).astype(BF16)
+    column_wait(*sums_z)
+    along = jnp.sum(sum_z[...], axis=0)
+    old_rows = along[:, 2:3]
+    sum_p[gy] = three(along[:, 0:1], along[:, 1:2], total(jnp.sum(row_out[...], axis=0, keepdims=True)))
+    sums_p = (sum_p, sp_ss, sp_rs)
+    small_start(*sums_p)
     for k, g in enumerate(peers):
         copy = remote(ph1, ph1_in.at[g], p1_ss.at[k], p1_rs.at[g], pdev(g))
         copy.wait_send()
@@ -536,12 +550,6 @@
     turned = [jnp.transpose(pair[:, i * 128:(i + 1) * 128]) for i in range(wide_feats // 128)]
     factors = (turned[0] if len(turned) == 1 else jnp.concatenate(turned, axis=0))[:feats]
 
-    column_wait(*sums_z)
-    along = jnp.sum(sum_z[...], axis=0)
-    old_rows = along[:, 2:3]
-    sum_p[gy] = three(along[:, 0:1], along[:, 1:2], total(jnp.sum(row_out[...], axis=0, keepdims=True)))
-    sums_p = (sum_p, sp_ss, sp_rs)
-    small_start(*sums_p)
     chips_wait(col_h, col_z, co_ss, co_rs)
     col_z[z] = col_h[...]
     col_o[core] = jnp.sum(col_z[...].astype(F32), axis=0)

time: 112 us -> 112 us (level)
  no operation moved by 1% of the time
where the time goes in v4:
time: 112 us
  Pallas kernels  111 us (99%)
    pallas_call x1, Pallas kernels, exchange(): pl.pallas_call(functools.partial(kernel, n_gx, n_gy, d_model), out_shape=...  110 us

profile of v4, /device:TPU:1, one launch (start us, length us, event | category | flops | bytes accessed | tf_op | source)
XLA Modules:
  0.0 111.8 jit_solution(9496346917174687193)
XLA Ops:
  0.6 109.5 %block_step.1 = (bf16[32,192]{1,0:T(8,128)(2,1)S(1)}, f32[32,192]{1,0:T(8,128)S(1)}, f32[192,1536]{1,0:T(8,128)S(1)}, f32[192,1536]{1,0:T(8,128)S(1)}, f32[8,128]{1,0:T(8,128)S(1)}) custom-call(bf16[32,192]{1,0:T(8,128)(2,1)} %patches_h.1, f32[1,192]{1,0:T(1,128)} %bitcast.10, bf16[32,192]{1,0:T(8,128)(2,1)} %upstream_h.1, bf16[192,1536]{1,0:T(8,128)(2,1)} %w_in_h.1, ...), custom_call_target="tpu_custom_call" | custom-call | tf_op jit(solution)/shard_map/block_step/pallas_call | solution.py:632
  110.2 1.6 %scale_updates.1 = (bf16[32,192]{1,0:T(8,128)(2,1)}, f32[32,192]{1,0:T(8,128)}, f32[192,1536]{1,0:T(8,128)}, f32[192,1536]{1,0:T(8,128)}) custom-call(bf16[32,192]{1,0:T(8,128)(2,1)S(1)} %get-tuple-element.13.output, f32[32,192]{1,0:T(8,128)S(1)} %get-tuple-element.14.input_grad, f32[192,1536]{1,0:T(8,128)S(1)} %get-tuple-element.15.grad_in, ...), custom_call_target="tpu_custom_call" | custom-call | tf_op jit(solution)/shard_map/scale_updates/pallas_call | solution.py:671
